TPU v7x, 256 devices: a whole 4x4x8 slice. The times are simulated.
256 devices in a mesh: patch: 128 (over x, z, y), strip: 2 (over core).
Axes of the slice: x: 4, y: 4, z: 8, core: 2. Of those that a mesh axis runs over, the one named last changes fastest.
Arguments:
- features: float32 [262144, 128], P(('patch', 'strip')), may hold values from -6 to 6
- lap_tiles: float32 [4096, 6, 4096], P(('patch', 'strip')), may hold values from -0.3125 to 0.3125
- columns: int32 [4096, 6], P(('patch', 'strip')), may hold values from 0 to 4095, as said below
- weights: float32 [3, 64, 64], replicated, may hold values from -0.75 to 0.75
- bias_term: float32 [64], replicated, may hold values from -4 to 4
- cotangent: float32 [262144, 128], P(('patch', 'strip')), may hold values from -6 to 6
Outputs:
- output: float32 [262144, 128], P(('patch', 'strip'))
- input_grad: float32 [262144, 128], P(('patch', 'strip'))
- weight_grad: float32 [3, 64, 64], replicated
- bias_grad: float32 [64], replicated
Inputs may be any that keep to these rules, and one draw needn't show every extreme that they name: `columns`: entry 0 of a block's 6 entries is the block itself and entry 1 lies exactly 4 blocks before or after it; all entries of a block are distinct blocks within 4 of it in the cyclic order of the 4096 blocks.
All inputs are finite; a program needn't handle non-finite values.
Results may differ from a plain program's by a relative error of at most 0.0001.
Values sent between devices are 32-bit elements; how exact they have to be, the bound alone decides.
No kernel may reach another device: no remote copies, remote signals or barrier semaphores. Data moves between devices by JAX's collectives and lax.ppermute only.
A program may use at most 64 MiB of HBM per device.

v0:
```python
import math

import jax
import jax.numpy as jnp
from jax import lax
from jax.experimental import pallas as pl
from jax.experimental.pallas import tpu as pltpu
from jax.sharding import Mesh
from jax.sharding import PartitionSpec as P

C = 64
BATCH = 2
PB = 64
NB = 6
HB = 4
BLK_DEV = 16
ROWS = BLK_DEV * PB
RIM = HB * PB
EXT = BLK_DEV + 2 * HB
W2 = BATCH * C
CHUNKS = PB * PB // 128
AXES = ("patch_0", "patch_1", "patch_2", "strip")
SHAPE = (4, 8, 4, 2)
BLOCKS = 4096
F32 = jnp.float32
BF16 = jnp.bfloat16
VMEM = pl.BlockSpec(memory_space=pltpu.VMEM)
SMEM = pl.BlockSpec(memory_space=pltpu.SMEM)
ANY = pl.BlockSpec(memory_space=pl.ANY)


def split(value):
    high = value.astype(BF16)
    return high, (value - high.astype(F32)).astype(BF16)


def mm(a, b):
    return jnp.dot(a, b, preferred_element_type=F32)


def mm_tn(a, b):
    return lax.dot_general(a, b, (((0,), (0,)), ((), ())), preferred_element_type=F32)


def slot_of(cols, b, j):
    return jnp.bitwise_and(cols[b, j] - cols[0, 0] + HB, BLOCKS - 1)


def is_first_core(cols):
    return jnp.bitwise_and(cols[0, 0] // BLK_DEV, 1) == 0


def rim_rows(cols):
    first = is_first_core(cols)
    low, high = 0, (BLK_DEV + HB) * PB
    return (
        pl.multiple_of(jnp.where(first, high, low), RIM),
        pl.multiple_of(jnp.where(first, low, high), RIM),
    )


def even_odd(ref, b):
    return jnp.concatenate(
        [ref[pl.ds(b * PB, PB // 2, stride=2), :], ref[pl.ds(b * PB + 1, PB // 2, stride=2), :]],
        axis=0,
    )


def spread(cols, at_ref, vec_ref, acc):
    def one(b, carry):
        high, low = split(even_odd(vec_ref, b))
        rhs = jnp.concatenate([high, high, low, low], axis=0)
        at = at_ref[b]
        out = mm(jnp.concatenate([at, at], axis=1), rhs)
        for j in range(NB):
            rows = pl.ds(pl.multiple_of(slot_of(cols, b, j) * PB, PB), PB)
            acc[rows, :] = acc[rows, :] + out[j * PB : (j + 1) * PB]
        return carry

    lax.fori_loop(0, BLK_DEV, one, 0, unroll=4)


def hop(cols, fa_ref, cat, out_ref):
    def one(b, carry):
        rhs = jnp.concatenate(
            [
                cat[pl.ds(pl.multiple_of(slot_of(cols, b, j) * PB, PB), PB), :]
                for j in range(NB)
            ],
            axis=0,
        )
        out = mm(fa_ref[b], rhs)
        out = out[:, :W2] + out[:, W2:]
        out = out[:PB] + out[PB:]
        out_ref[pl.ds(b * PB, PB // 2, stride=2), :] = out[: PB // 2]
        out_ref[pl.ds(b * PB + 1, PB // 2, stride=2), :] = out[PB // 2 :]
        return carry

    lax.fori_loop(0, BLK_DEV, one, 0, unroll=4)


def put_cat(cat, start, value):
    high, low = split(value)
    cat[pl.ds(start, value.shape[0]), :] = jnp.concatenate([high, low], axis=1)


def build_kernel(cols, tiles, g_ref, fa_ref, at_ref, u_ref, send_a, send_b, raw, acc, sem):
    copies = [
        pltpu.make_async_copy(
            tiles.at[:, :, pl.ds(k * 128, 128)], raw.at[:, pl.ds(8 * k, NB), :], sem.at[k]
        )
        for k in range(CHUNKS)
    ]
    for copy in copies:
        copy.start()
    acc[...] = jnp.zeros_like(acc)
    for copy in copies:
        copy.wait()
    low_lanes = lax.broadcasted_iota(jnp.int32, (CHUNKS, 128), 1) < PB

    def one(b, carry):
        for pair in range(NB // 2):
            even = raw[b, pl.ds(2 * pair, CHUNKS, stride=8), :]
            odd = raw[b, pl.ds(2 * pair + 1, CHUNKS, stride=8), :]
            top = jnp.where(low_lanes, even, pltpu.roll(odd, PB, 1))
            bottom = jnp.where(low_lanes, pltpu.roll(even, PB, 1), odd)
            both = jnp.concatenate([top, bottom], axis=0)
            high = both.astype(BF16)
            rest = both - high.astype(F32)
            low = rest.astype(BF16)
            lanes = pl.ds(pair * 128, 128)
            stacked = jnp.concatenate([high, low], axis=0)
            fa_ref[b, :, lanes] = stacked
            at_ref[b, lanes, :] = stacked.astype(F32).T.astype(BF16)
        return carry

    lax.fori_loop(0, BLK_DEV, one, 0, unroll=4)
    spread(cols, at_ref, g_ref, acc)
    u_ref[...] = acc[RIM : RIM + ROWS, :]
    row_a, row_b = rim_rows(cols)
    send_a[...] = acc[pl.ds(row_a, RIM), :]
    send_b[...] = acc[pl.ds(row_b, RIM), :]


def maps_sum(full):
    return full[:C] + pltpu.roll(full[C:], C, 1)


def first_kernel(cols, fa_ref, x_ref, x_a, x_b, g_ref, u_ref, first_ref, grads_ref, cat, *, scale):
    row_a, row_b = rim_rows(cols)
    put_cat(cat, RIM, x_ref[...])
    put_cat(cat, row_a, x_a[...])
    put_cat(cat, row_b, x_b[...])
    hop(cols, fa_ref, cat, first_ref)
    g_high, g_low = split(g_ref[...])
    u_high, u_low = split(u_ref[...])
    f_high, f_low = split(first_ref[...])
    xs = cat[RIM : RIM + ROWS, :]
    gs = jnp.concatenate([g_high, g_low], axis=1)
    gus = jnp.concatenate([g_high, g_low, u_high, u_low], axis=1)
    zero = mm_tn(xs, gs)
    zero = zero[:W2] + zero[W2:]
    zero = zero[:, :W2] + zero[:, W2:]
    rest = mm_tn(jnp.concatenate([f_high, f_low], axis=1), gus)
    rest = rest[:W2] + rest[W2:]
    one = rest[:, :W2] + rest[:, W2 : 2 * W2]
    two = 2.0 * (rest[:, 2 * W2 : 3 * W2] + rest[:, 3 * W2 :]) - zero
    low_lanes = lax.broadcasted_iota(jnp.int32, (C, 128), 1) < C
    zero, one, two = maps_sum(zero), maps_sum(one), maps_sum(two)
    grads_ref[0:C, :] = scale * jnp.where(low_lanes, zero, pltpu.roll(one, C, 1))
    half = C // 2
    grads_ref[C : C + half, :] = scale * jnp.where(
        low_lanes[:half], two[:half], pltpu.roll(two[half:], C, 1)
    )
    bias = jnp.sum(g_ref[...], axis=0, keepdims=True)
    grads_ref[C + half : C + half + 8, :] = jnp.broadcast_to(
        scale * (bias + pltpu.roll(bias, C, 1)), (8, 128)
    )


def grads_kernel(cols, first_ref, u_a, u_b, part_ref, grads_ref, *, scale):
    row_a, row_b = rim_rows(cols)
    total = jnp.zeros((W2, W2), F32)
    for row, u in ((row_a, u_a), (row_b, u_b)):
        own = pl.multiple_of(jnp.where(row == 0, 0, ROWS - RIM), RIM)
        f_high, f_low = split(first_ref[pl.ds(own, RIM), :])
        u_high, u_low = split(u[...])
        out = mm_tn(
            jnp.concatenate([f_high, f_low], axis=1), jnp.concatenate([u_high, u_low], axis=1)
        )
        out = out[:W2] + out[W2:]
        total = total + out[:, :W2] + out[:, W2:]
    two = (2.0 * scale) * maps_sum(total)
    half = C // 2
    low_lanes = lax.broadcasted_iota(jnp.int32, (half, 128), 1) < C
    grads_ref[...] = part_ref[...]
    grads_ref[C : C + half, :] = part_ref[C : C + half, :] + jnp.where(
        low_lanes, two[:half], pltpu.roll(two[half:], C, 1)
    )


def both_maps(weight):
    zero = jnp.zeros_like(weight)
    return jnp.concatenate(
        [jnp.concatenate([weight, zero], axis=1), jnp.concatenate([zero, weight], axis=1)], axis=0
    )


def mixed(value, weight):
    high, low = split(value)
    w_high, w_low = split(weight)
    row = jnp.concatenate([w_high, w_low], axis=1)
    out = mm(jnp.concatenate([high, low], axis=1), jnp.concatenate([row, row], axis=0))
    return out[:, :W2] + out[:, W2:]


def inner_kernel(
    cols, at_ref, g_ref, u_ref, u_a, u_b, w_ref, first_ref, u2_ref, send_a, send_b, inner, acc
):
    row_a, row_b = rim_rows(cols)
    inner[...] = u_ref[...]
    for row, u in ((row_a, u_a), (row_b, u_b)):
        own = pl.multiple_of(jnp.where(row == 0, 0, ROWS - RIM), RIM)
        inner[pl.ds(own, RIM), :] = inner[pl.ds(own, RIM), :] + u[...]
    inner[...] = mixed(g_ref[...], both_maps(w_ref[1]).T) + 2.0 * mixed(
        inner[...], both_maps(w_ref[2]).T
    )
    acc[...] = jnp.zeros_like(acc)
    spread(cols, at_ref, inner, acc)
    u2_ref[...] = acc[RIM : RIM + ROWS, :]
    for row, send in ((row_a, send_a), (row_b, send_b)):
        own = pl.multiple_of(jnp.where(row == 0, 0, ROWS - RIM), RIM)
        send[0:RIM, :] = first_ref[pl.ds(own, RIM), :]
        send[RIM : 2 * RIM, :] = acc[pl.ds(row, RIM), :]


def last_kernel(
    cols, fa_ref, x_ref, g_ref, first_ref, u2_ref, r_a, r_b, w_ref, bias_ref,
    out_ref, back_ref, cat, second,
):
    row_a, row_b = rim_rows(cols)
    put_cat(cat, RIM, first_ref[...])
    put_cat(cat, row_a, r_a[0:RIM, :])
    put_cat(cat, row_b, r_b[0:RIM, :])
    hop(cols, fa_ref, cat, second)
    x = x_ref[...]
    two = 2.0 * second[...] - x
    bias = bias_ref[...]
    out_ref[...] = (
        mixed(x, both_maps(w_ref[0]))
        + mixed(first_ref[...], both_maps(w_ref[1]))
        + mixed(two, both_maps(w_ref[2]))
        + jnp.concatenate([bias, bias], axis=1)
    )
    g = g_ref[...]
    back_ref[...] = u2_ref[...] + mixed(g, both_maps(w_ref[0] - w_ref[2]).T)
    for row, r in ((row_a, r_a), (row_b, r_b)):
        own = pl.multiple_of(jnp.where(row == 0, 0, ROWS - RIM), RIM)
        back_ref[pl.ds(own, RIM), :] = back_ref[pl.ds(own, RIM), :] + r[RIM : 2 * RIM, :]


def call(kernel, name, out, specs, scratch, flops, moved):
    return pl.pallas_call(
        kernel,
        name=name,
        out_shape=[jax.ShapeDtypeStruct(s, d) for s, d in out],
        in_specs=specs,
        out_specs=[VMEM] * len(out),
        scratch_shapes=scratch,
        compiler_params=pltpu.CompilerParams(vmem_limit_bytes=32 * 1024 * 1024),
        cost_estimate=pl.CostEstimate(flops=flops, bytes_accessed=moved, transcendentals=0),
    )


def index(a, b, c, s):
    return ((a * SHAPE[1] + b) * SHAPE[2] + c) * SHAPE[3] + s


def place(i):
    return (i // 64, (i // 8) % 8, (i // 2) % 4, i % 2)


COUNT = 256
IN_CHIP = [(i, i ^ 1) for i in range(COUNT)]
CROSS = [(i, (i + 1) % COUNT) if i % 2 else (i, (i - 1) % COUNT) for i in range(COUNT)]
RING4 = ((1, 0, 3, 2), (3, 2, 1, 0))
RING8 = ((1, 0, 3, 2, 5, 4, 7, 6), (7, 2, 1, 4, 3, 6, 5, 0), (3, 6, 5, 0, 7, 2, 1, 4))


def moves():
    steps = [IN_CHIP]
    for table in RING4:
        steps.append([(i, index(a, b, table[c], s)) for i, (a, b, c, s) in enumerate(map(place, range(COUNT)))])
    for table in RING4:
        steps.append([(i, index(table[a], b, c, s)) for i, (a, b, c, s) in enumerate(map(place, range(COUNT)))])
    for table in RING8:
        steps.append([(i, index(a, table[b], c, s)) for i, (a, b, c, s) in enumerate(map(place, range(COUNT)))])
    return steps


def shards(features, lap_tiles, columns, weights, bias_term, cotangent):
    scale = 1.0 / math.sqrt(BATCH * PB * BLOCKS)
    first_core = lax.axis_index("strip") == 0
    x_a = lax.dynamic_slice_in_dim(features, jnp.where(first_core, ROWS - RIM, 0), RIM, 0)
    x_b = lax.dynamic_slice_in_dim(features, jnp.where(first_core, 0, ROWS - RIM), RIM, 0)
    x_b = lax.ppermute(x_b, AXES, CROSS)
    x_a = lax.ppermute(x_a, AXES, IN_CHIP)
    field = ((ROWS, W2), F32)
    rim = ((RIM, W2), F32)
    fa, at, u, u_a, u_b = call(
        build_kernel, "build",
        [((BLK_DEV, 2 * PB, NB * PB), BF16), ((BLK_DEV, NB * PB, 2 * PB), BF16), field, rim, rim],
        [SMEM, ANY, VMEM],
        [
            pltpu.VMEM((BLK_DEV, CHUNKS * 8, 128), F32),
            pltpu.VMEM((EXT * PB, W2), F32),
            pltpu.SemaphoreType.DMA((CHUNKS,)),
        ],
        800_000_000, 8_000_000,
    )(columns, lap_tiles, cotangent)
    u_b = lax.ppermute(u_b, AXES, CROSS)
    u_a = lax.ppermute(u_a, AXES, IN_CHIP)

    def first_body(*refs):
        first_kernel(*refs, scale=scale)

    first, part = call(
        first_body, "first", [field, ((C + C // 2 + 8, W2), F32)],
        [SMEM] + [VMEM] * 6, [pltpu.VMEM((EXT * PB, 2 * W2), BF16)], 800_000_000, 4_000_000,
    )(columns, fa, features, x_a, x_b, cotangent, u)

    def grads_body(*refs):
        grads_kernel(*refs, scale=scale)

    (grads,) = call(
        grads_body, "grads", [((C + C // 2 + 8, W2), F32)], [SMEM] + [VMEM] * 4, [],
        50_000_000, 500_000,
    )(columns, first, u_a, u_b, part)
    for step in moves()[:1]:
        grads = grads + lax.ppermute(grads, AXES, step)
    u2, s_a, s_b = call(
        inner_kernel, "inner", [field, ((2 * RIM, W2), F32), ((2 * RIM, W2), F32)],
        [SMEM] + [VMEM] * 7,
        [pltpu.VMEM((ROWS, W2), F32), pltpu.VMEM((EXT * PB, W2), F32)], 800_000_000, 4_000_000,
    )(columns, at, cotangent, u, u_a, u_b, weights, first)
    s_b = lax.ppermute(s_b, AXES, CROSS)
    s_a = lax.ppermute(s_a, AXES, IN_CHIP)
    output, input_grad = call(
        last_kernel, "last", [field, field], [SMEM] + [VMEM] * 9,
        [pltpu.VMEM((EXT * PB, 2 * W2), BF16), pltpu.VMEM((ROWS, W2), F32)],
        800_000_000, 5_000_000,
    )(columns, fa, features, cotangent, first, u2, s_a, s_b, weights, bias_term.reshape(1, C))
    for step in moves()[1:]:
        grads = grads + lax.ppermute(grads, AXES, step)
    half = C // 2
    weight_grad = jnp.stack(
        [
            grads[:C, :C],
            grads[:C, C:],
            jnp.concatenate([grads[C : C + half, :C], grads[C : C + half, C:]], axis=0),
        ]
    )
    return output, input_grad, weight_grad, grads[C + half, :C]


def solution(mesh):
    grid = Mesh(mesh.devices.reshape(*SHAPE), AXES)
    placed = (P(AXES, None), P(AXES, None, None), P(AXES, None), P(), P(), P(AXES, None))
    return jax.shard_map(
        shards,
        mesh=grid,
        in_specs=placed,
        out_specs=(P(AXES, None), P(AXES, None), P(), P()),
        check_vma=False,
    )
```

profile of v0, /device:TPU:32, one launch (start us, length us, event | category | flops | bytes accessed | tf_op | source)
XLA Modules:
  0.0 69.9 jit_solution(2621855909357647113)
XLA Ops:
  0.6 1.0 %constant_dynamic-slice_fusion = (f32[256,128]{1,0:T(8,128)S(1)}, f32[256,128]{1,0:T(8,128)S(1)}) fusion(f32[1024,128]{1,0:T(8,128)} %x_ref.1, s32[]{:T(128)S(6)} %select_n.10, s32[]{:T(128)S(6)} %select_n.9), kind=kLoop, calls=%fused_computation.5 | loop fusion | bytes 524296 | tf_op jit(solution)/shard_map/dynamic_slice | solution.py:305
  1.6 0.1 collective-permute-start
  1.7 2.7 %collective-permute-start.1 = (f32[256,128]{1,0:T(8,128)S(1)}, f32[256,128]{1,0:T(8,128)S(1)}, u32[]{:S(2)}, u32[]{:S(2)}) collective-permute-start(f32[256,128]{1,0:T(8,128)S(1)} %get-tuple-element.28), channel_id=1, source_target_pairs={{0,255},{1,2},{2,1},{3,4},{4,3},{5,6},{6,5},{7,8},{8,7},{9,10},{10... | collective-permute-start | bytes 393224 | tf_op jit(solution)/shard_map/ppermute | solution.py:306
  4.4 0.8 %copy.14.cols.refs_0_ = s32[16,6]{1,0:T(8,128)S(1)} copy(s32[16,6]{0,1:T(8,128)} %param.8) | data formatting | bytes 768 | tf_op args[2]
  5.2 2.4 %copy.11.tiles = f32[16,6,4096]{2,1,0:T(8,128)S(1)} copy(f32[16,6,4096]{2,0,1:T(8,128)} %param.7) | data formatting | bytes 3145728 | tf_op args[1]
  7.6 4.8 %build.1 = (bf16[16,128,384]{2,1,0:T(8,128)(2,1)S(1)}, bf16[16,384,128]{2,1,0:T(8,128)(2,1)S(1)}, f32[1024,128]{1,0:T(8,128)S(1)}, f32[256,128]{1,0:T(8,128)S(1)}, f32[256,128]{1,0:T(8,128)S(1)}) custom-call(s32[16,6]{1,0:T(8,128)S(1)} %copy.14.cols.refs_0_, f32[16,6,4096]{2,1,0:T(8,128)S(1)} %copy.11.tiles, f32[1024,128]{1,0:T(8,128)S(1)} %copy-done), custom_call_target="tpu_custom_call" | custom-call | flops 800000000 | bytes 8000000 | tf_op jit(solution)/shard_map/build/pallas_call | solution.py:310
  12.4 0.1 collective-permute-start.2
  12.5 1.4 %collective-permute-start.3 = (f32[256,128]{1,0:T(8,128)S(1)}, f32[256,128]{1,0:T(8,128)S(1)}, u32[]{:S(2)}, u32[]{:S(2)}) collective-permute-start(f32[256,128]{1,0:T(8,128)S(1)} %get-tuple-element.21), channel_id=1, source_target_pairs={{0,255},{1,2},{2,1},{3,4},{4,3},{5,6},{6,5},{7,8},{8,7},{9,10},{10... | collective-permute-start | bytes 393224 | tf_op jit(solution)/shard_map/ppermute | solution.py:321
  13.9 2.8 %first.1 = (f32[1024,128]{1,0:T(8,128)S(1)}, f32[104,128]{1,0:T(8,128)S(1)}) custom-call(s32[16,6]{1,0:T(8,128)S(1)} %copy.14.cols.refs_0_, bf16[16,128,384]{2,1,0:T(8,128)(2,1)S(1)} %get-tuple-element.16.refs_1_.fa_ref, f32[1024,128]{1,0:T(8,128)S(1)} %copy-done.1, f32[256,128]{1,0:T(8,128)S(1)} %collective-permute-done.refs_3_, ...), custom_call_target="tpu_custom_call" | custom-call | flops 800000000 | bytes 4000000 | tf_op jit(solution)/shard_map/first/pallas_call | solution.py:327
  16.7 2.4 %collective-permute-done.3.u_b.refs_3_ = f32[256,128]{1,0:T(8,128)S(1)} collective-permute-done((f32[256,128]{1,0:T(8,128)S(1)}, f32[256,128]{1,0:T(8,128)S(1)}, u32[]{:S(2)}, u32[]{:S(2)}) %collective-permute-start.3) | collective-permute-done | bytes 131104 | tf_op jit(solution)/shard_map/ppermute | solution.py:321
  19.1 1.1 %grads.1 = f32[104,128]{1,0:T(8,128)S(1)} custom-call(s32[16,6]{1,0:T(8,128)S(1)} %copy.14.cols.refs_0_, f32[1024,128]{1,0:T(8,128)S(1)} %get-tuple-element.18.first_ref.refs_1_, f32[256,128]{1,0:T(8,128)S(1)} %collective-permute-done.2.u_a.refs_2_, f32[256,128]{1,0:T(8,128)S(1)} %collective-permute-done.3.u_b.refs_3_, f32[104,128]{1,0:T(8,128)S(1)} %get-tuple-element.27.refs_4_), custom_call_target="tpu_custom_call" | custom-call | flops 50000000 | bytes 500000 | tf_op jit(solution)/shard_map/grads/pallas_call | solution.py:335
  20.2 1.2 %collective-permute-done.6 = f32[104,128]{1,0:T(8,128)S(1)} collective-permute-done((f32[104,128]{1,0:T(8,128)S(1)}, f32[104,128]{1,0:T(8,128)S(1)}, u32[]{:S(2)}, u32[]{:S(2)}) %collective-permute-start.6) | collective-permute-done | bytes 53280 | tf_op jit(solution)/shard_map/ppermute | solution.py:340
  21.5 0.1 collective-permute-start.7
  21.6 4.1 %collective-permute-done.7 = f32[104,128]{1,0:T(8,128)S(1)} collective-permute-done((f32[104,128]{1,0:T(8,128)S(1)}, f32[104,128]{1,0:T(8,128)S(1)}, u32[]{:S(2)}, u32[]{:S(2)}) %collective-permute-start.7) | collective-permute-done | bytes 53280 | tf_op jit(solution)/shard_map/ppermute | solution.py:354
  25.7 1.8 %collective-permute-start.8 = (f32[104,128]{1,0:T(8,128)S(1)}, f32[104,128]{1,0:T(8,128)S(1)}, u32[]{:S(2)}, u32[]{:S(2)}) collective-permute-start(f32[104,128]{1,0:T(8,128)S(1)} %add.27), channel_id=1, source_target_pairs={{0,6},{1,7},{2,4},{3,5},{4,2},{5,3},{6,0},{7,1},{8,14},{9,15},{10,... | collective-permute-start | bytes 159752 | tf_op jit(solution)/shard_map/ppermute | solution.py:354
  27.5 3.0 %inner.1 = (f32[1024,128]{1,0:T(8,128)S(1)}, f32[512,128]{1,0:T(8,128)S(1)}, f32[512,128]{1,0:T(8,128)S(1)}) custom-call(s32[16,6]{1,0:T(8,128)S(1)} %copy.14.cols.refs_0_, bf16[16,384,128]{2,1,0:T(8,128)(2,1)S(1)} %get-tuple-element.19.at_ref, f32[1024,128]{1,0:T(8,128)S(1)} %copy-done, f32[1024,128]{1,0:T(8,128)S(1)} %get-tuple-element.17.refs_6_.u_ref, ...), custom_call_target="tpu_custom_call" | custom-call | flops 800000000 | bytes 4000000 | tf_op jit(solution)/shard_map/inner/pallas_call | solution.py:341
  30.5 0.1 collective-permute-start.4
  30.6 12.4 %collective-permute-start.5 = (f32[512,128]{1,0:T(8,128)S(1)}, f32[512,128]{1,0:T(8,128)S(1)}, u32[]{:S(2)}, u32[]{:S(2)}) collective-permute-start(f32[512,128]{1,0:T(8,128)S(1)} %get-tuple-element.24), channel_id=1, source_target_pairs={{0,255},{1,2},{2,1},{3,4},{4,3},{5,6},{6,5},{7,8},{8,7},{9,10},{10... | collective-permute-start | bytes 786440 | tf_op jit(solution)/shard_map/ppermute | solution.py:346
  43.0 0.1 collective-permute-start.9
  43.1 4.1 %collective-permute-done.9 = f32[104,128]{1,0:T(8,128)S(1)} collective-permute-done((f32[104,128]{1,0:T(8,128)S(1)}, f32[104,128]{1,0:T(8,128)S(1)}, u32[]{:S(2)}, u32[]{:S(2)}) %collective-permute-start.9) | collective-permute-done | bytes 53280 | tf_op jit(solution)/shard_map/ppermute | solution.py:354
  47.3 0.1 collective-permute-start.10
  47.4 5.3 %collective-permute-done.10 = f32[104,128]{1,0:T(8,128)S(1)} collective-permute-done((f32[104,128]{1,0:T(8,128)S(1)}, f32[104,128]{1,0:T(8,128)S(1)}, u32[]{:S(2)}, u32[]{:S(2)}) %collective-permute-start.10) | collective-permute-done | bytes 53280 | tf_op jit(solution)/shard_map/ppermute | solution.py:354
  52.7 0.1 collective-permute-start.11
  52.8 4.3 %collective-permute-done.11 = f32[104,128]{1,0:T(8,128)S(1)} collective-permute-done((f32[104,128]{1,0:T(8,128)S(1)}, f32[104,128]{1,0:T(8,128)S(1)}, u32[]{:S(2)}, u32[]{:S(2)}) %collective-permute-start.11) | collective-permute-done | bytes 53280 | tf_op jit(solution)/shard_map/ppermute | solution.py:354
  57.1 0.1 collective-permute-start.12
  57.2 4.1 %collective-permute-done.12 = f32[104,128]{1,0:T(8,128)S(1)} collective-permute-done((f32[104,128]{1,0:T(8,128)S(1)}, f32[104,128]{1,0:T(8,128)S(1)}, u32[]{:S(2)}, u32[]{:S(2)}) %collective-permute-start.12) | collective-permute-done | bytes 53280 | tf_op jit(solution)/shard_map/ppermute | solution.py:354
  61.3 0.1 collective-permute-start.13
  61.5 3.9 %last.1 = (f32[1024,128]{1,0:T(8,128)}, f32[1024,128]{1,0:T(8,128)}) custom-call(s32[16,6]{1,0:T(8,128)S(1)} %copy.14.cols.refs_0_, bf16[16,128,384]{2,1,0:T(8,128)(2,1)S(1)} %get-tuple-element.16.refs_1_.fa_ref, f32[1024,128]{1,0:T(8,128)S(1)} %copy-done.1, f32[1024,128]{1,0:T(8,128)S(1)} %copy-done, f32[1024,128]{1,0:T(8,128)S(1)} %get-tuple-element.18.first_ref.refs_1_, ...), custom_call_target="tpu_custom_call" | custom-call | flops 800000000 | bytes 5000000 | tf_op jit(solution)/shard_map/last/pallas_call | solution.py:348
  65.4 3.2 %collective-permute-done.13 = f32[104,128]{1,0:T(8,128)S(1)} collective-permute-done((f32[104,128]{1,0:T(8,128)S(1)}, f32[104,128]{1,0:T(8,128)S(1)}, u32[]{:S(2)}, u32[]{:S(2)}) %collective-permute-start.13) | collective-permute-done | bytes 53280 | tf_op jit(solution)/shard_map/ppermute | solution.py:354
  68.6 0.1 slice_bitcast_fusion.1
  68.8 0.5 slice_bitcast_fusion.2
  69.3 0.7 pad_maximum_fusion
  (25 shorter events, 0.2 us)
Async XLA Ops:
  1.6 12.3 %collective-permute-start = (f32[256,128]{1,0:T(8,128)S(1)}, f32[256,128]{1,0:T(8,128)S(1)}, u32[]{:S(2)}, u32[]{:S(2)}) collective-permute-start(f32[256,128]{1,0:T(8,128)S(1)} %get-tuple-element.29), channel_id=1, source_target_pairs={{0,1},{1,0},{2,3},{3,2},{4,5},{5,4},{6,7},{7,6},{8,9},{9,8},{10,11... | collective-permute-start | bytes 393224 | tf_op jit(solution)/shard_map/ppermute | solution.py:307
  1.7 12.2 %collective-permute-start.1 = (f32[256,128]{1,0:T(8,128)S(1)}, f32[256,128]{1,0:T(8,128)S(1)}, u32[]{:S(2)}, u32[]{:S(2)}) collective-permute-start(f32[256,128]{1,0:T(8,128)S(1)} %get-tuple-element.28), channel_id=1, source_target_pairs={{0,255},{1,2},{2,1},{3,4},{4,3},{5,6},{6,5},{7,8},{8,7},{9,10},{10... | collective-permute-start | bytes 393224 | tf_op jit(solution)/shard_map/ppermute | solution.py:306
  5.2 2.4 %copy-start = (f32[1024,128]{1,0:T(8,128)S(1)}, f32[1024,128]{1,0:T(8,128)}, u32[]{:S(2)}) copy-start(f32[1024,128]{1,0:T(8,128)} %g_ref.5) | copy-start | bytes 1572868
  7.6 6.3 %copy-start.1 = (f32[1024,128]{1,0:T(8,128)S(1)}, f32[1024,128]{1,0:T(8,128)}, u32[]{:S(2)}) copy-start(f32[1024,128]{1,0:T(8,128)} %x_ref.1) | copy-start | bytes 1572868
  12.4 4.3 %collective-permute-start.2 = (f32[256,128]{1,0:T(8,128)S(1)}, f32[256,128]{1,0:T(8,128)S(1)}, u32[]{:S(2)}, u32[]{:S(2)}) collective-permute-start(f32[256,128]{1,0:T(8,128)S(1)} %get-tuple-element.20), channel_id=1, source_target_pairs={{0,1},{1,0},{2,3},{3,2},{4,5},{5,4},{6,7},{7,6},{8,9},{9,8},{10,11... | collective-permute-start | bytes 393224 | tf_op jit(solution)/shard_map/ppermute | solution.py:322
  12.5 6.6 %collective-permute-start.3 = (f32[256,128]{1,0:T(8,128)S(1)}, f32[256,128]{1,0:T(8,128)S(1)}, u32[]{:S(2)}, u32[]{:S(2)}) collective-permute-start(f32[256,128]{1,0:T(8,128)S(1)} %get-tuple-element.21), channel_id=1, source_target_pairs={{0,255},{1,2},{2,1},{3,4},{4,3},{5,6},{6,5},{7,8},{8,7},{9,10},{10... | collective-permute-start | bytes 393224 | tf_op jit(solution)/shard_map/ppermute | solution.py:321
  13.9 13.6 %copy-start.2 = (f32[3,64,64]{2,1,0:T(8,128)S(1)}, f32[3,64,64]{2,1,0:T(8,128)}, u32[]{:S(2)}) copy-start(f32[3,64,64]{2,1,0:T(8,128)} %w_ref.3) | copy-start | bytes 147460
  20.2 1.3 %collective-permute-start.6 = (f32[104,128]{1,0:T(8,128)S(1)}, f32[104,128]{1,0:T(8,128)S(1)}, u32[]{:S(2)}, u32[]{:S(2)}) collective-permute-start(f32[104,128]{1,0:T(8,128)S(1)} %grads.1), channel_id=1, source_target_pairs={{0,1},{1,0},{2,3},{3,2},{4,5},{5,4},{6,7},{7,6},{8,9},{9,8},{10,11... | collective-permute-start | bytes 159752 | tf_op jit(solution)/shard_map/ppermute | solution.py:340
  21.5 4.2 %collective-permute-start.7 = (f32[104,128]{1,0:T(8,128)S(1)}, f32[104,128]{1,0:T(8,128)S(1)}, u32[]{:S(2)}, u32[]{:S(2)}) collective-permute-start(f32[104,128]{1,0:T(8,128)S(1)} %add.26), channel_id=1, source_target_pairs={{0,2},{1,3},{2,0},{3,1},{4,6},{5,7},{6,4},{7,5},{8,10},{9,11},{10,... | collective-permute-start | bytes 159752 | tf_op jit(solution)/shard_map/ppermute | solution.py:354
  25.7 17.3 %collective-permute-start.8 = (f32[104,128]{1,0:T(8,128)S(1)}, f32[104,128]{1,0:T(8,128)S(1)}, u32[]{:S(2)}, u32[]{:S(2)}) collective-permute-start(f32[104,128]{1,0:T(8,128)S(1)} %add.27), channel_id=1, source_target_pairs={{0,6},{1,7},{2,4},{3,5},{4,2},{5,3},{6,0},{7,1},{8,14},{9,15},{10,... | collective-permute-start | bytes 159752 | tf_op jit(solution)/shard_map/ppermute | solution.py:354
  27.5 33.9 %copy-start.3 = (f32[64]{0:T(128)S(1)}, f32[64]{0:T(128)}, u32[]{:S(2)}) copy-start(f32[64]{0:T(128)} %param.10) | copy-start | bytes 772
  30.5 31.0 %collective-permute-start.4 = (f32[512,128]{1,0:T(8,128)S(1)}, f32[512,128]{1,0:T(8,128)S(1)}, u32[]{:S(2)}, u32[]{:S(2)}) collective-permute-start(f32[512,128]{1,0:T(8,128)S(1)} %get-tuple-element.23), channel_id=1, source_target_pairs={{0,1},{1,0},{2,3},{3,2},{4,5},{5,4},{6,7},{7,6},{8,9},{9,8},{10,11... | collective-permute-start | bytes 786440 | tf_op jit(solution)/shard_map/ppermute | solution.py:347
  30.6 30.9 %collective-permute-start.5 = (f32[512,128]{1,0:T(8,128)S(1)}, f32[512,128]{1,0:T(8,128)S(1)}, u32[]{:S(2)}, u32[]{:S(2)}) collective-permute-start(f32[512,128]{1,0:T(8,128)S(1)} %get-tuple-element.24), channel_id=1, source_target_pairs={{0,255},{1,2},{2,1},{3,4},{4,3},{5,6},{6,5},{7,8},{8,7},{9,10},{10... | collective-permute-start | bytes 786440 | tf_op jit(solution)/shard_map/ppermute | solution.py:346
  43.0 4.2 %collective-permute-start.9 = (f32[104,128]{1,0:T(8,128)S(1)}, f32[104,128]{1,0:T(8,128)S(1)}, u32[]{:S(2)}, u32[]{:S(2)}) collective-permute-start(f32[104,128]{1,0:T(8,128)S(1)} %add.28), channel_id=1, source_target_pairs={{0,64},{1,65},{2,66},{3,67},{4,68},{5,69},{6,70},{7,71},{8,72},{9,... | collective-permute-start | bytes 159752 | tf_op jit(solution)/shard_map/ppermute | solution.py:354
  47.3 5.4 %collective-permute-start.10 = (f32[104,128]{1,0:T(8,128)S(1)}, f32[104,128]{1,0:T(8,128)S(1)}, u32[]{:S(2)}, u32[]{:S(2)}) collective-permute-start(f32[104,128]{1,0:T(8,128)S(1)} %add.29), channel_id=1, source_target_pairs={{0,192},{1,193},{2,194},{3,195},{4,196},{5,197},{6,198},{7,199},{8... | collective-permute-start | bytes 159752 | tf_op jit(solution)/shard_map/ppermute | solution.py:354
  52.7 4.4 %collective-permute-start.11 = (f32[104,128]{1,0:T(8,128)S(1)}, f32[104,128]{1,0:T(8,128)S(1)}, u32[]{:S(2)}, u32[]{:S(2)}) collective-permute-start(f32[104,128]{1,0:T(8,128)S(1)} %add.30), channel_id=1, source_target_pairs={{0,8},{1,9},{2,10},{3,11},{4,12},{5,13},{6,14},{7,15},{8,0},{9,1},... | collective-permute-start | bytes 159752 | tf_op jit(solution)/shard_map/ppermute | solution.py:354
  57.1 4.2 %collective-permute-start.12 = (f32[104,128]{1,0:T(8,128)S(1)}, f32[104,128]{1,0:T(8,128)S(1)}, u32[]{:S(2)}, u32[]{:S(2)}) collective-permute-start(f32[104,128]{1,0:T(8,128)S(1)} %add.31), channel_id=1, source_target_pairs={{0,56},{1,57},{2,58},{3,59},{4,60},{5,61},{6,62},{7,63},{8,16},{9,... | collective-permute-start | bytes 159752 | tf_op jit(solution)/shard_map/ppermute | solution.py:354
  61.3 7.3 %collective-permute-start.13 = (f32[104,128]{1,0:T(8,128)S(1)}, f32[104,128]{1,0:T(8,128)S(1)}, u32[]{:S(2)}, u32[]{:S(2)}) collective-permute-start(f32[104,128]{1,0:T(8,128)S(1)} %add.32), channel_id=1, source_target_pairs={{0,24},{1,25},{2,26},{3,27},{4,28},{5,29},{6,30},{7,31},{8,48},{9,... | collective-permute-start | bytes 159752 | tf_op jit(solution)/shard_map/ppermute | solution.py:354
where the time goes:
time: 70.1 us; the launch traced here: 69.9 us
  waiting for transfers between devices  28.8 us (41%)
  starting transfers between devices  19.2 us (27%)
  Pallas kernels  15.5 us (22%)
  local copies, waits for them, and re-layouts  4.85 us (7%)
  between operations  0.83 us (1%)
  other arithmetic  0.73 us (1%)
    ppermute x8, waiting for transfers between devices, shards(): grads = grads + lax.ppermute(grads, AXES, step)  26.4 us
    ppermute x1, starting transfers between devices, shards(): s_b = lax.ppermute(s_b, AXES, CROSS)  12.4 us
    pallas_call x1, Pallas kernels, shards(): call(build_kernel, 'build', [((BLK_DEV, 2 * PB, NB * PB), BF16), ((BLK_DE...  4.81 us
    pallas_call x1, Pallas kernels, shards(): call(last_kernel, 'last', [field, field], [SMEM] + [VMEM] * 9, [pltpu.VME...  3.89 us
    unnamed x10, local copies, waits for them, and re-layouts  3.2 us
    pallas_call x1, Pallas kernels, shards(): call(inner_kernel, 'inner', [field, ((2 * RIM, W2), F32), ((2 * RIM, W2),...  2.95 us
    pallas_call x1, Pallas kernels, shards(): call(first_body, 'first', [field, ((C + C // 2 + 8, W2), F32)], [SMEM] +...  2.8 us
    ppermute x1, starting transfers between devices, shards(): x_b = lax.ppermute(x_b, AXES, CROSS)  2.66 us
  transfers between devices with their start and end apart: 14, of which 8 were waited for; matrix products, arithmetic and copies ran while one was open for 5% of the time, Pallas kernels for 21%

commit v1 on v0

v1 whole, which is shorter than its diff:
```python
import math

import jax
import jax.numpy as jnp
from jax import lax
from jax.experimental import pallas as pl
from jax.experimental.pallas import tpu as pltpu
from jax.sharding import Mesh
from jax.sharding import PartitionSpec as P

C = 64
BATCH = 2
PB = 64
NB = 6
HB = 4
BLK_DEV = 16
ROWS = BLK_DEV * PB
RIM = HB * PB
EXT = BLK_DEV + 2 * HB
MID = BLK_DEV - 2 * HB
W2 = BATCH * C
CHUNKS = PB * PB // 128
AXES = ("patch_0", "patch_1", "patch_2", "strip")
SHAPE = (4, 8, 4, 2)
BLOCKS = 4096
F32 = jnp.float32
BF16 = jnp.bfloat16
VMEM = pl.BlockSpec(memory_space=pltpu.VMEM)
SMEM = pl.BlockSpec(memory_space=pltpu.SMEM)
HBM = pl.BlockSpec(memory_space=pltpu.HBM)


def split(value):
    high = value.astype(BF16)
    return high, (value - high.astype(F32)).astype(BF16)


def mm(a, b):
    return jnp.dot(a, b, preferred_element_type=F32)


def mm_tn(a, b):
    return lax.dot_general(a, b, (((0,), (0,)), ((), ())), preferred_element_type=F32)


def slot_of(cols, b, j):
    return jnp.bitwise_and(cols[b, j] - cols[0, 0] + HB, BLOCKS - 1)


def is_first_core(cols):
    return jnp.bitwise_and(cols[0, 0] // BLK_DEV, 1) == 0


def rim_rows(cols):
    first = is_first_core(cols)
    low, high = 0, (BLK_DEV + HB) * PB
    return (
        pl.multiple_of(jnp.where(first, high, low), RIM),
        pl.multiple_of(jnp.where(first, low, high), RIM),
    )


def rim_half(row):
    return pl.multiple_of(jnp.where(row == 0, 0, RIM), RIM)


def rim_block(i):
    return jnp.where(i < HB, i, i + MID)


def mid_block(i):
    return i + HB


def block_rows(ref, i):
    return jnp.concatenate(
        [ref[pl.ds(i * PB, PB // 2, stride=2), :], ref[pl.ds(i * PB + 1, PB // 2, stride=2), :]],
        axis=0,
    )


def rows_of(slot):
    return pl.ds(pl.multiple_of(slot * PB, PB), PB)


def spread(cols, at_ref, vec_ref, acc, block):
    def one(i, carry):
        b = block(i)
        high, low = split(block_rows(vec_ref, i))
        rhs = jnp.concatenate([high, high, low, low], axis=0)
        at = at_ref[i]
        out = mm(jnp.concatenate([at, at], axis=1), rhs)
        for j in range(NB):
            rows = rows_of(slot_of(cols, b, j))
            acc[rows, :] = acc[rows, :] + out[j * PB : (j + 1) * PB]
        return carry

    lax.fori_loop(0, MID, one, 0, unroll=4)


def hop(cols, fa_ref, cat, out_ref, block):
    def one(i, carry):
        b = block(i)
        rhs = jnp.concatenate([cat[rows_of(slot_of(cols, b, j)), :] for j in range(NB)], axis=0)
        out = mm(fa_ref[i], rhs)
        out = out[:, :W2] + out[:, W2:]
        out = out[:PB] + out[PB:]
        out_ref[pl.ds(i * PB, PB // 2, stride=2), :] = out[: PB // 2]
        out_ref[pl.ds(i * PB + 1, PB // 2, stride=2), :] = out[PB // 2 :]
        return carry

    lax.fori_loop(0, MID, one, 0, unroll=4)


def put_cat(cat, start, value):
    high, low = split(value)
    cat[pl.ds(start, value.shape[0]), :] = jnp.concatenate([high, low], axis=1)


def build(raw, fa_ref, at_ref):
    low_lanes = lax.broadcasted_iota(jnp.int32, (CHUNKS, 128), 1) < PB

    def one(i, carry):
        for pair in range(NB // 2):
            even = raw[i, pl.ds(2 * pair, CHUNKS, stride=8), :]
            odd = raw[i, pl.ds(2 * pair + 1, CHUNKS, stride=8), :]
            top = jnp.where(low_lanes, even, pltpu.roll(odd, PB, 1))
            bottom = jnp.where(low_lanes, pltpu.roll(even, PB, 1), odd)
            both = jnp.concatenate([top, bottom], axis=0)
            high = both.astype(BF16)
            low = (both - high.astype(F32)).astype(BF16)
            lanes = pl.ds(pair * 128, 128)
            stacked = jnp.concatenate([high, low], axis=0)
            fa_ref[i, :, lanes] = stacked
            at_ref[i, lanes, :] = stacked.astype(F32).T.astype(BF16)
        return carry

    lax.fori_loop(0, MID, one, 0, unroll=4)


def tile_copies(tiles, raw, sem, pieces):
    return [
        pltpu.make_async_copy(
            tiles.at[pl.ds(start, count), :, pl.ds(k * 128, 128)],
            raw.at[pl.ds(at, count), pl.ds(8 * k, NB), :],
            sem.at[n * CHUNKS + k],
        )
        for n, (start, count, at) in enumerate(pieces)
        for k in range(CHUNKS)
    ]


def rim_kernel(
    cols_hbm, tiles, g_hbm, x_hbm,
    cols_ref, fa_ref, at_ref, acc, send_a, send_b,
    cols, raw, g_rim, x_rim, sem, small,
):
    to_cols = pltpu.make_async_copy(cols_hbm, cols, small.at[0])
    others = [pltpu.make_async_copy(cols_hbm, cols_ref, small.at[1])]
    for n, (value, to) in enumerate(((g_hbm, g_rim), (x_hbm, x_rim))):
        others.append(
            pltpu.make_async_copy(value.at[pl.ds(0, RIM)], to.at[pl.ds(0, RIM)], small.at[2 + 2 * n])
        )
        others.append(
            pltpu.make_async_copy(
                value.at[pl.ds(ROWS - RIM, RIM)], to.at[pl.ds(RIM, RIM)], small.at[3 + 2 * n]
            )
        )
    copies = tile_copies(tiles, raw, sem, ((0, HB, 0), (BLK_DEV - HB, HB, HB)))
    for copy in copies + [to_cols] + others:
        copy.start()
    acc[...] = jnp.zeros_like(acc)
    for copy in copies:
        copy.wait()
    build(raw, fa_ref, at_ref)
    to_cols.wait()
    for copy in others:
        copy.wait()
    spread(cols, at_ref, g_rim, acc, rim_block)
    for row, send in zip(rim_rows(cols), (send_a, send_b)):
        send[0:RIM, :] = x_rim[pl.ds(rim_half(row), RIM), :]
        send[RIM : 2 * RIM, :] = acc[pl.ds(row, RIM), :]


def maps_sum(full):
    return full[:C] + pltpu.roll(full[C:], C, 1)


def products(left, right):
    a = jnp.concatenate([h for value in left for h in split(value)], axis=1)
    b = jnp.concatenate([h for value in right for h in split(value)], axis=1)
    out = mm_tn(a, b)
    result = []
    for p in range(len(left)):
        band = out[2 * p * W2 : (2 * p + 1) * W2] + out[(2 * p + 1) * W2 : (2 * p + 2) * W2]
        result.append(
            [
                band[:, 2 * q * W2 : (2 * q + 1) * W2] + band[:, (2 * q + 1) * W2 : (2 * q + 2) * W2]
                for q in range(len(right))
            ]
        )
    return result


def packed(zero, one, two):
    low_lanes = lax.broadcasted_iota(jnp.int32, (C, 128), 1) < C
    two = maps_sum(two)
    one = pltpu.roll(maps_sum(one), C, 1)
    if zero is None:
        top = jnp.where(low_lanes, 0.0, one)
    else:
        top = jnp.where(low_lanes, maps_sum(zero), one)
    bottom = jnp.where(low_lanes[: C // 2], two[: C // 2], pltpu.roll(two[C // 2 :], C, 1))
    return jnp.concatenate([top, bottom], axis=0)


def both_maps(weight):
    zero = jnp.zeros_like(weight)
    return jnp.concatenate(
        [jnp.concatenate([weight, zero], axis=1), jnp.concatenate([zero, weight], axis=1)], axis=0
    )


def mixed(value, weight):
    high, low = split(value)
    w_high, w_low = split(weight)
    row = jnp.concatenate([w_high, w_low], axis=1)
    out = mm(jnp.concatenate([high, low], axis=1), jnp.concatenate([row, row], axis=0))
    return out[:, :W2] + out[:, W2:]


def mid_kernel(
    cols, tiles, g_ref, x_ref, acc_in, w_ref,
    fa_ref, at_ref, first_ref, u_rim, part_ref, acc,
    raw, cat, inner, u_mid, sem, *, scale,
):
    copies = tile_copies(tiles, raw, sem, ((HB, MID, 0),))
    for copy in copies:
        copy.start()
    put_cat(cat, RIM, x_ref[...])
    acc[...] = acc_in[...]
    for copy in copies:
        copy.wait()
    build(raw, fa_ref, at_ref)
    g_mid = g_ref.at[pl.ds(RIM, MID * PB)]
    spread(cols, at_ref, g_mid, acc, mid_block)
    u_mid[...] = acc[2 * RIM : 4 * RIM, :]
    u_rim[0:RIM, :] = acc[RIM : 2 * RIM, :]
    u_rim[RIM : 2 * RIM, :] = acc[4 * RIM : 5 * RIM, :]
    hop(cols, fa_ref, cat, first_ref, mid_block)
    inner[...] = mixed(g_mid[...], both_maps(w_ref[1]).T) + 2.0 * mixed(
        u_mid[...], both_maps(w_ref[2]).T
    )
    acc[...] = jnp.zeros_like(acc)
    spread(cols, at_ref, inner, acc, mid_block)
    ((zero,),) = products([x_ref[...]], [g_ref[...]])
    ((one, two),) = products([first_ref[...]], [g_mid[...], u_mid[...]])
    part_ref[0 : C + C // 2, :] = scale * packed(zero, one, 2.0 * two - zero)
    bias = scale * jnp.sum(g_ref[...], axis=0, keepdims=True)
    part_ref[C + C // 2 :, :] = jnp.broadcast_to(bias + pltpu.roll(bias, C, 1), (8, 128))


def meet_kernel(
    cols, fa_ref, x_ref, r_a, r_b, g_ref, u_part, part_ref, first_ref, u_ref, grads_ref, cat, *, scale
):
    put_cat(cat, RIM, x_ref[...])
    for row, r in zip(rim_rows(cols), (r_a, r_b)):
        put_cat(cat, row, r[0:RIM, :])
        half = pl.ds(rim_half(row), RIM)
        u_ref[half, :] = u_part[half, :] + r[RIM : 2 * RIM, :]
    hop(cols, fa_ref, cat, first_ref, rim_block)
    g_rim = jnp.concatenate([g_ref[0:RIM, :], g_ref[ROWS - RIM :, :]], axis=0)
    ((one, two),) = products([first_ref[...]], [g_rim, u_ref[...]])
    size = C + C // 2
    grads_ref[0:size, :] = part_ref[0:size, :] + scale * packed(None, one, 2.0 * two)
    grads_ref[size:, :] = part_ref[size:, :]


def inner_kernel(
    cols, at_ref, g_ref, u_ref, w_ref, first_ref, acc_in, u2_ref, send_a, send_b, inner, acc
):
    g_rim = jnp.concatenate([g_ref[0:RIM, :], g_ref[ROWS - RIM :, :]], axis=0)
    inner[...] = mixed(g_rim, both_maps(w_ref[1]).T) + 2.0 * mixed(
        u_ref[...], both_maps(w_ref[2]).T
    )
    acc[...] = acc_in[...]
    spread(cols, at_ref, inner, acc, rim_block)
    u2_ref[...] = acc[RIM : RIM + ROWS, :]
    for row, send in zip(rim_rows(cols), (send_a, send_b)):
        send[0:RIM, :] = first_ref[pl.ds(rim_half(row), RIM), :]
        send[RIM : 2 * RIM, :] = acc[pl.ds(row, RIM), :]


def outputs(x, g, one, hopped, w_ref, bias_ref):
    bias = bias_ref[...]
    out = (
        mixed(x, both_maps(w_ref[0]))
        + mixed(one, both_maps(w_ref[1]))
        + mixed(2.0 * hopped - x, both_maps(w_ref[2]))
        + jnp.concatenate([bias, bias], axis=1)
    )
    return out, mixed(g, both_maps(w_ref[0] - w_ref[2]).T)


def last_mid_kernel(
    cols, fa_ref, x_ref, g_ref, f_mid, f_rim, u2_ref, w_ref, bias_ref, out_ref, back_ref, cat, second
):
    put_cat(cat, RIM, f_rim[0:RIM, :])
    put_cat(cat, 2 * RIM, f_mid[...])
    put_cat(cat, 4 * RIM, f_rim[RIM : 2 * RIM, :])
    hop(cols, fa_ref, cat, second, mid_block)
    mid = slice(RIM, ROWS - RIM)
    out, back = outputs(x_ref[mid, :], g_ref[mid, :], f_mid[...], second[...], w_ref, bias_ref)
    out_ref[...] = out
    back_ref[...] = back + u2_ref[mid, :]


def last_rim_kernel(
    cols, fa_ref, x_ref, g_ref, f_mid, f_rim, r_a, r_b, u2_ref, w_ref, bias_ref, o_mid, b_mid,
    out_ref, back_ref, cat, second,
):
    put_cat(cat, RIM, f_rim[0:RIM, :])
    put_cat(cat, 2 * RIM, f_mid[...])
    put_cat(cat, 4 * RIM, f_rim[RIM : 2 * RIM, :])
    for row, r in zip(rim_rows(cols), (r_a, r_b)):
        put_cat(cat, row, r[0:RIM, :])
    hop(cols, fa_ref, cat, second, rim_block)
    x = jnp.concatenate([x_ref[0:RIM, :], x_ref[ROWS - RIM :, :]], axis=0)
    g = jnp.concatenate([g_ref[0:RIM, :], g_ref[ROWS - RIM :, :]], axis=0)
    out, back = outputs(x, g, f_rim[...], second[...], w_ref, bias_ref)
    mid = slice(RIM, ROWS - RIM)
    out_ref[mid, :] = o_mid[...]
    back_ref[mid, :] = b_mid[...]
    for at, half in ((0, 0), (ROWS - RIM, RIM)):
        out_ref[at : at + RIM, :] = out[half : half + RIM]
        back_ref[at : at + RIM, :] = back[half : half + RIM] + u2_ref[at : at + RIM, :]
    for row, r in zip(rim_rows(cols), (r_a, r_b)):
        own = pl.ds(pl.multiple_of(jnp.where(row == 0, 0, ROWS - RIM), RIM), RIM)
        back_ref[own, :] = back_ref[own, :] + r[RIM : 2 * RIM, :]


def final_kernel(mine, theirs, weight_ref, bias_ref):
    total = mine[...] + theirs[...]
    half = C // 2
    weight_ref[0] = total[:C, :C]
    weight_ref[1] = pltpu.roll(total[:C], C, 1)[:, :C]
    weight_ref[2, 0:half, :] = total[C : C + half, :C]
    weight_ref[2, half:C, :] = pltpu.roll(total[C : C + half], C, 1)[:, :C]
    bias_ref[...] = total[C + half : C + half + 1, :C]


def call(kernel, name, out, specs, scratch, flops, moved):
    return pl.pallas_call(
        kernel,
        name=name,
        out_shape=[jax.ShapeDtypeStruct(s, d) for s, d in out],
        in_specs=specs,
        out_specs=[VMEM] * len(out),
        scratch_shapes=scratch,
        compiler_params=pltpu.CompilerParams(vmem_limit_bytes=24 * 1024 * 1024),
        cost_estimate=pl.CostEstimate(flops=flops, bytes_accessed=moved, transcendentals=0),
    )


def index(a, b, c, s):
    return ((a * SHAPE[1] + b) * SHAPE[2] + c) * SHAPE[3] + s


def place(i):
    return (i // 64, (i // 8) % 8, (i // 2) % 4, i % 2)


COUNT = 256
IN_CHIP = [(i, i ^ 1) for i in range(COUNT)]
CROSS = [(i, (i + 1) % COUNT) if i % 2 else (i, (i - 1) % COUNT) for i in range(COUNT)]
RING4 = ((1, 0, 3, 2), (3, 2, 1, 0))
RING8 = ((1, 0, 3, 2, 5, 4, 7, 6), (7, 2, 1, 4, 3, 6, 5, 0), (3, 6, 5, 0, 7, 2, 1, 4))


def moves():
    steps = [IN_CHIP]
    for table in RING4:
        steps.append([(i, index(a, b, table[c], s)) for i, (a, b, c, s) in enumerate(map(place, range(COUNT)))])
    for table in RING4:
        steps.append([(i, index(table[a], b, c, s)) for i, (a, b, c, s) in enumerate(map(place, range(COUNT)))])
    for table in RING8:
        steps.append([(i, index(a, table[b], c, s)) for i, (a, b, c, s) in enumerate(map(place, range(COUNT)))])
    return steps


def shards(features, lap_tiles, columns, weights, bias_term, cotangent):
    scale = 1.0 / math.sqrt(BATCH * PB * BLOCKS)
    field = ((ROWS, W2), F32)
    half = ((ROWS // 2, W2), F32)
    extended = ((EXT * PB, W2), F32)
    sums = ((C + C // 2 + 8, W2), F32)
    natural = ((MID, 2 * PB, NB * PB), BF16)
    turned = ((MID, NB * PB, 2 * PB), BF16)
    raw = pltpu.VMEM((MID, CHUNKS * 8, 128), F32)
    cat = pltpu.VMEM((EXT * PB, 2 * W2), BF16)
    half_scratch = pltpu.VMEM((ROWS // 2, W2), F32)

    def scaled(kernel):
        def body(*refs):
            kernel(*refs, scale=scale)

        return body

    cols, fa_rim, at_rim, acc, s_a, s_b = call(
        rim_kernel, "rim", [((BLK_DEV, NB), jnp.int32), natural, turned, extended, half, half],
        [HBM] * 4,
        [
            pltpu.SMEM((BLK_DEV, NB), jnp.int32), raw, half_scratch, half_scratch,
            pltpu.SemaphoreType.DMA((2 * CHUNKS,)), pltpu.SemaphoreType.DMA((6,)),
        ],
        400_000_000, 4_000_000,
    )(columns, lap_tiles, cotangent, features)
    r_b = lax.ppermute(s_b, AXES, CROSS)
    r_a = lax.ppermute(s_a, AXES, IN_CHIP)
    fa_mid, at_mid, f_mid, u_rim, part, acc = call(
        scaled(mid_kernel), "mid", [natural, turned, half, half, sums, extended],
        [SMEM, HBM] + [VMEM] * 4,
        [raw, cat, half_scratch, half_scratch, pltpu.SemaphoreType.DMA((CHUNKS,))],
        1_600_000_000, 9_000_000,
    )(cols, lap_tiles, cotangent, features, acc, weights)
    f_rim, u_rim, grads = call(
        scaled(meet_kernel), "meet", [half, half, sums], [SMEM] + [VMEM] * 7, [cat],
        400_000_000, 3_000_000,
    )(cols, fa_rim, features, r_a, r_b, cotangent, u_rim, part)
    steps = moves()
    grads = grads + lax.ppermute(grads, AXES, steps[0])
    u2, s_a, s_b = call(
        inner_kernel, "inner", [field, half, half], [SMEM] + [VMEM] * 6,
        [half_scratch, pltpu.VMEM(*extended)], 400_000_000, 3_000_000,
    )(cols, at_rim, cotangent, u_rim, weights, f_rim, acc)
    s_b = lax.ppermute(s_b, AXES, CROSS)
    s_a = lax.ppermute(s_a, AXES, IN_CHIP)
    bias_row = bias_term.reshape(1, C)
    o_mid, b_mid = call(
        last_mid_kernel, "last_mid", [half, half], [SMEM] + [VMEM] * 8, [cat, half_scratch],
        600_000_000, 4_000_000,
    )(cols, fa_mid, features, cotangent, f_mid, f_rim, u2, weights, bias_row)
    output, input_grad = call(
        last_rim_kernel, "last_rim", [field, field], [SMEM] + [VMEM] * 12, [cat, half_scratch],
        600_000_000, 5_000_000,
    )(cols, fa_rim, features, cotangent, f_mid, f_rim, s_a, s_b, u2, weights, bias_row, o_mid, b_mid)
    for step in steps[1:-1]:
        grads = grads + lax.ppermute(grads, AXES, step)
    weight_grad, bias_grad = call(
        final_kernel, "final", [((3, C, C), F32), ((1, C), F32)], [VMEM, VMEM], [], 1000, 100_000
    )(grads, lax.ppermute(grads, AXES, steps[-1]))
    return output, input_grad, weight_grad, bias_grad.reshape(C)


def solution(mesh):
    grid = Mesh(mesh.devices.reshape(*SHAPE), AXES)
    placed = (P(AXES, None), P(AXES, None, None), P(AXES, None), P(), P(), P(AXES, None))
    return jax.shard_map(
        shards,
        mesh=grid,
        in_specs=placed,
        out_specs=(P(AXES, None), P(AXES, None), P(), P()),
        check_vma=False,
    )
```

time: 70.1 us -> 63.7 us (0.909)
  waiting for transfers between devices: 28.8 us -> 22.5 us
  Pallas kernels: 15.5 us -> 19.2 us
  local copies, waits for them, and re-layouts: 4.85 us -> 3.22 us
  starting transfers between devices: 19.2 us -> 17.8 us
    ppermute x8 -> x6, waiting for transfers between devices: 26.4 us -> 17.1 us  [shards(): grads = grads + lax.ppermute(grads, AXES, step)]
    ppermute x1, starting transfers between devices: 12.4 us -> 8.74 us  [shards(): s_b = lax.ppermute(s_b, AXES, CROSS)]
    ppermute x8 -> x6, starting transfers between devices: 2.42 us -> 6.04 us  [shards(): grads = grads + lax.ppermute(grads, AXES, step)]
    pallas_call x5 -> x7, Pallas kernels: 15.5 us -> 19.2 us  [the longest x1 6.25 us: shards(): call(scaled(mid_kernel), 'mid', [natural, turned, half, half, sums, exten...]
    ppermute x4, waiting for transfers between devices: 2.38 us -> 5.36 us  [the longest x1 4.13 us: shards(): lax.ppermute(grads, AXES, steps[-1])]
    ppermute x4, starting transfers between devices: 4.22 us -> 2.94 us  [the longest x1 2.67 us: shards(): r_b = lax.ppermute(s_b, AXES, CROSS)]
    dynamic_slice x1 -> x0, local copies, waits for them, and re-layouts: 0.99 us -> none  [shards(): lax.dynamic_slice_in_dim(features, jnp.where(first_core, 0, ROWS - RIM),...]
  transfers between devices with their start and end apart: 14 -> 12, of which waited for: 8 -> 7; matrix products, arithmetic and copies ran while one was open for 5% -> 0% of each run, Pallas kernels for 21% -> 21%
where the time goes in v1:
time: 63.7 us; the launch traced here: 63.6 us
  waiting for transfers between devices  22.5 us (35%)
  Pallas kernels  19.2 us (30%)
  starting transfers between devices  17.8 us (28%)
  local copies, waits for them, and re-layouts  3.22 us (5%)
  between operations  0.82 us (1%)
    ppermute x6, waiting for transfers between devices, shards(): grads = grads + lax.ppermute(grads, AXES, step)  17.1 us
    ppermute x1, starting transfers between devices, shards(): s_b = lax.ppermute(s_b, AXES, CROSS)  8.74 us
    pallas_call x1, Pallas kernels, shards(): call(scaled(mid_kernel), 'mid', [natural, turned, half, half, sums, exten...  6.25 us
    ppermute x6, starting transfers between devices, shards(): grads = grads + lax.ppermute(grads, AXES, step)  6.04 us
    ppermute x1, waiting for transfers between devices, shards(): lax.ppermute(grads, AXES, steps[-1])  4.13 us
    pallas_call x1, Pallas kernels, shards(): call(rim_kernel, 'rim', [((BLK_DEV, NB), jnp.int32), natural, turned, ext...  3.4 us
    unnamed x10, local copies, waits for them, and re-layouts  3.22 us
    pallas_call x1, Pallas kernels, shards(): call(last_rim_kernel, 'last_rim', [field, field], [SMEM] + [VMEM] * 12, [...  2.99 us
  transfers between devices with their start and end apart: 12, of which 7 were waited for; matrix products, arithmetic and copies ran while one was open for 0% of the time, Pallas kernels for 21%

profile of v1, /device:TPU:32, one launch (start us, length us, event | category | flops | bytes accessed | tf_op | source)
XLA Modules:
  0.0 63.6 jit_solution(6261531307177287106)
XLA Ops:
  0.7 0.8 %copy.10.cols_hbm = s32[16,6]{1,0:T(8,128)S(1)} copy(s32[16,6]{0,1:T(8,128)} %param.8) | data formatting | bytes 768 | tf_op args[2]
  1.5 2.4 %copy.11.tiles.refs_1_ = f32[16,6,4096]{2,1,0:T(8,128)S(1)} copy(f32[16,6,4096]{2,0,1:T(8,128)} %param.7) | data formatting | bytes 3145728 | tf_op args[1]
  3.9 0.0 copy-start.2
  3.9 3.4 %rim.1 = (s32[16,6]{1,0:T(8,128)S(1)}, bf16[8,128,384]{2,1,0:T(8,128)(2,1)S(1)}, bf16[8,384,128]{2,1,0:T(8,128)(2,1)S(1)}, f32[1536,128]{1,0:T(8,128)S(1)}, f32[...) custom-call(s32[16,6]{1,0:T(8,128)S(1)} %copy.10.cols_hbm, f32[16,6,4096]{2,1,0:T(8,128)S(1)} %copy.11.tiles.refs_1_, ...), custom_call_target="tpu_custom_call" | custom-call | flops 400000000 | bytes 4000000 | tf_op jit(solution)/shard_map/rim/pallas_call | solution.py:409
  7.3 0.1 collective-permute-start
  7.4 2.7 %collective-permute-start.1 = (f32[512,128]{1,0:T(8,128)S(1)}, f32[512,128]{1,0:T(8,128)S(1)}, u32[]{:S(2)}, u32[]{:S(2)}) collective-permute-start(f32[512,128]{1,0:T(8,128)S(1)} %get-tuple-element.32), channel_id=1, source_target_pairs={{0,255},{1,2},{2,1},{3,4},{4,3},{5,6},{6,5},{7,8},{8,7},{9,10},{10... | collective-permute-start | bytes 786440 | tf_op jit(solution)/shard_map/ppermute | solution.py:418
  10.1 6.3 %mid.1 = (bf16[8,128,384]{2,1,0:T(8,128)(2,1)S(1)}, bf16[8,384,128]{2,1,0:T(8,128)(2,1)}, f32[512,128]{1,0:T(8,128)S(1)}, f32[512,128]{1,0:T(8,128)S(1)}, f32[10...) custom-call(s32[16,6]{1,0:T(8,128)S(1)} %get-tuple-element.27.refs_0_.cols, f32[16,6,4096]{2,1,0:T(8,128)S(1)} %copy.11.tiles.refs_1_, ...), custom_call_target="tpu_custom_call" | custom-call | flops 1600000000 | bytes 9000000 | tf_op jit(solution)/shard_map/mid/pallas_call | solution.py:420
  16.3 0.0 collective-permute-done.refs_3_
  16.3 0.0 collective-permute-done.1.refs_4_
  16.3 1.9 %meet.1 = (f32[512,128]{1,0:T(8,128)S(1)}, f32[512,128]{1,0:T(8,128)S(1)}, f32[104,128]{1,0:T(8,128)S(1)}) custom-call(s32[16,6]{1,0:T(8,128)S(1)} %get-tuple-element.27.refs_0_.cols, bf16[8,128,384]{2,1,0:T(8,128)(2,1)S(1)} %get-tuple-element.28.refs_1_.fa_ref, f32[1024,128]{1,0:T(8,128)S(1)} %copy-done.1, f32[512,128]{1,0:T(8,128)S(1)} %collective-permute-done.refs_3_, ...), custom_call_target="tpu_custom_call" | custom-call | flops 400000000 | bytes 3000000 | tf_op jit(solution)/shard_map/meet/pallas_call | solution.py:426
  18.3 0.0 copy-start.3
  18.3 0.1 collective-permute-start.4
  18.4 1.2 %collective-permute-done.4 = f32[104,128]{1,0:T(8,128)S(1)} collective-permute-done((f32[104,128]{1,0:T(8,128)S(1)}, f32[104,128]{1,0:T(8,128)S(1)}, u32[]{:S(2)}, u32[]{:S(2)}) %collective-permute-start.4) | collective-permute-done | bytes 53280 | tf_op jit(solution)/shard_map/ppermute | solution.py:431
  19.6 0.4 collective-permute-start.5
  20.0 3.8 %collective-permute-done.5 = f32[104,128]{1,0:T(8,128)S(1)} collective-permute-done((f32[104,128]{1,0:T(8,128)S(1)}, f32[104,128]{1,0:T(8,128)S(1)}, u32[]{:S(2)}, u32[]{:S(2)}) %collective-permute-start.5) | collective-permute-done | bytes 53280 | tf_op jit(solution)/shard_map/ppermute | solution.py:448
  23.8 2.2 %collective-permute-start.6 = (f32[104,128]{1,0:T(8,128)S(1)}, f32[104,128]{1,0:T(8,128)S(1)}, u32[]{:S(2)}, u32[]{:S(2)}) collective-permute-start(f32[104,128]{1,0:T(8,128)S(1)} %add.22), channel_id=1, source_target_pairs={{0,6},{1,7},{2,4},{3,5},{4,2},{5,3},{6,0},{7,1},{8,14},{9,15},{10,... | collective-permute-start | bytes 159752 | tf_op jit(solution)/shard_map/ppermute | solution.py:448
  26.0 2.0 %inner.1 = (f32[1024,128]{1,0:T(8,128)S(1)}, f32[512,128]{1,0:T(8,128)S(1)}, f32[512,128]{1,0:T(8,128)S(1)}) custom-call(s32[16,6]{1,0:T(8,128)S(1)} %get-tuple-element.27.refs_0_.cols, bf16[8,384,128]{2,1,0:T(8,128)(2,1)S(1)} %get-tuple-element.36.at_ref, f32[1024,128]{1,0:T(8,128)S(1)} %copy-done, f32[512,128]{1,0:T(8,128)S(1)} %get-tuple-element.37.u_ref, ...), custom_call_target="tpu_custom_call" | custom-call | flops 400000000 | bytes 3000000 | tf_op jit(solution)/shard_map/inner/pallas_call | solution.py:432
  28.0 0.1 collective-permute-start.2
  28.1 8.7 %collective-permute-start.3 = (f32[512,128]{1,0:T(8,128)S(1)}, f32[512,128]{1,0:T(8,128)S(1)}, u32[]{:S(2)}, u32[]{:S(2)}) collective-permute-start(f32[512,128]{1,0:T(8,128)S(1)} %get-tuple-element.40), channel_id=1, source_target_pairs={{0,255},{1,2},{2,1},{3,4},{4,3},{5,6},{6,5},{7,8},{8,7},{9,10},{10... | collective-permute-start | bytes 786440 | tf_op jit(solution)/shard_map/ppermute | solution.py:436
  36.9 0.1 collective-permute-start.7
  37.0 4.1 %collective-permute-done.7 = f32[104,128]{1,0:T(8,128)S(1)} collective-permute-done((f32[104,128]{1,0:T(8,128)S(1)}, f32[104,128]{1,0:T(8,128)S(1)}, u32[]{:S(2)}, u32[]{:S(2)}) %collective-permute-start.7) | collective-permute-done | bytes 53280 | tf_op jit(solution)/shard_map/ppermute | solution.py:448
  41.1 0.9 %collective-permute-start.8 = (f32[104,128]{1,0:T(8,128)S(1)}, f32[104,128]{1,0:T(8,128)S(1)}, u32[]{:S(2)}, u32[]{:S(2)}) collective-permute-start(f32[104,128]{1,0:T(8,128)S(1)} %add.24), channel_id=1, source_target_pairs={{0,192},{1,193},{2,194},{3,195},{4,196},{5,197},{6,198},{7,199},{8... | collective-permute-start | bytes 159752 | tf_op jit(solution)/shard_map/ppermute | solution.py:448
  42.0 4.5 %collective-permute-done.8 = f32[104,128]{1,0:T(8,128)S(1)} collective-permute-done((f32[104,128]{1,0:T(8,128)S(1)}, f32[104,128]{1,0:T(8,128)S(1)}, u32[]{:S(2)}, u32[]{:S(2)}) %collective-permute-start.8) | collective-permute-done | bytes 53280 | tf_op jit(solution)/shard_map/ppermute | solution.py:448
  46.5 2.4 %collective-permute-start.9 = (f32[104,128]{1,0:T(8,128)S(1)}, f32[104,128]{1,0:T(8,128)S(1)}, u32[]{:S(2)}, u32[]{:S(2)}) collective-permute-start(f32[104,128]{1,0:T(8,128)S(1)} %add.25), channel_id=1, source_target_pairs={{0,8},{1,9},{2,10},{3,11},{4,12},{5,13},{6,14},{7,15},{8,0},{9,1},... | collective-permute-start | bytes 159752 | tf_op jit(solution)/shard_map/ppermute | solution.py:448
  48.9 2.1 %collective-permute-done.9 = f32[104,128]{1,0:T(8,128)S(1)} collective-permute-done((f32[104,128]{1,0:T(8,128)S(1)}, f32[104,128]{1,0:T(8,128)S(1)}, u32[]{:S(2)}, u32[]{:S(2)}) %collective-permute-start.9) | collective-permute-done | bytes 53280 | tf_op jit(solution)/shard_map/ppermute | solution.py:448
  51.0 0.1 collective-permute-start.10
  51.1 1.9 %last_mid.1 = (f32[512,128]{1,0:T(8,128)S(1)}, f32[512,128]{1,0:T(8,128)S(1)}) custom-call(s32[16,6]{1,0:T(8,128)S(1)} %get-tuple-element.27.refs_0_.cols, bf16[8,128,384]{2,1,0:T(8,128)(2,1)S(1)} %get-tuple-element.42.fa_ref, f32[1024,128]{1,0:T(8,128)S(1)} %copy-done.1, f32[1024,128]{1,0:T(8,128)S(1)} %copy-done, f32[512,128]{1,0:T(8,128)S(1)} %get-tuple-element.30.f_mid, ...), custom_call_target="tpu_custom_call" | custom-call | flops 600000000 | bytes 4000000 | tf_op jit(solution)/shard_map/last_mid/pallas_call | solution.py:439
  53.1 2.6 %collective-permute-done.10 = f32[104,128]{1,0:T(8,128)S(1)} collective-permute-done((f32[104,128]{1,0:T(8,128)S(1)}, f32[104,128]{1,0:T(8,128)S(1)}, u32[]{:S(2)}, u32[]{:S(2)}) %collective-permute-start.10) | collective-permute-done | bytes 53280 | tf_op jit(solution)/shard_map/ppermute | solution.py:448
  55.6 0.1 collective-permute-start.11
  55.8 3.0 %last_rim.1 = (f32[1024,128]{1,0:T(8,128)}, f32[1024,128]{1,0:T(8,128)}) custom-call(s32[16,6]{1,0:T(8,128)S(1)} %get-tuple-element.27.refs_0_.cols, bf16[8,128,384]{2,1,0:T(8,128)(2,1)S(1)} %get-tuple-element.28.refs_1_.fa_ref, f32[1024,128]{1,0:T(8,128)S(1)} %copy-done.1, f32[1024,128]{1,0:T(8,128)S(1)} %copy-done, ...), custom_call_target="tpu_custom_call" | custom-call | flops 600000000 | bytes 5000000 | tf_op jit(solution)/shard_map/last_rim/pallas_call | solution.py:443
  58.7 4.1 %collective-permute-done.11.theirs = f32[104,128]{1,0:T(8,128)S(1)} collective-permute-done((f32[104,128]{1,0:T(8,128)S(1)}, f32[104,128]{1,0:T(8,128)S(1)}, u32[]{:S(2)}, u32[]{:S(2)}) %collective-permute-start.11) | collective-permute-done | bytes 53280 | tf_op jit(solution)/shard_map/ppermute | solution.py:451
  62.9 0.7 %final.1 = (f32[3,64,64]{2,1,0:T(8,128)}, f32[1,64]{1,0:T(1,128)}) custom-call(f32[104,128]{1,0:T(8,128)S(1)} %add.27.mine, f32[104,128]{1,0:T(8,128)S(1)} %collective-permute-done.11.theirs), custom_call_target="tpu_custom_call" | custom-call | flops 1000 | bytes 100000 | tf_op jit(solution)/shard_map/final/pallas_call | solution.py:449
  (16 shorter events, 0.1 us)
Async XLA Ops:
  0.6 3.2 %copy-start = (f32[1024,128]{1,0:T(8,128)S(1)}, f32[1024,128]{1,0:T(8,128)}, u32[]{:S(2)}) copy-start(f32[1024,128]{1,0:T(8,128)} %g_ref.5) | copy-start | bytes 1572868
  0.6 3.2 %copy-start.1 = (f32[1024,128]{1,0:T(8,128)S(1)}, f32[1024,128]{1,0:T(8,128)}, u32[]{:S(2)}) copy-start(f32[1024,128]{1,0:T(8,128)} %x_ref.3) | copy-start | bytes 1572868
  3.9 6.2 %copy-start.2 = (f32[3,64,64]{2,1,0:T(8,128)S(1)}, f32[3,64,64]{2,1,0:T(8,128)}, u32[]{:S(2)}) copy-start(f32[3,64,64]{2,1,0:T(8,128)} %w_ref.5) | copy-start | bytes 147460
  7.3 9.0 %collective-permute-start = (f32[512,128]{1,0:T(8,128)S(1)}, f32[512,128]{1,0:T(8,128)S(1)}, u32[]{:S(2)}, u32[]{:S(2)}) collective-permute-start(f32[512,128]{1,0:T(8,128)S(1)} %get-tuple-element.31), channel_id=1, source_target_pairs={{0,1},{1,0},{2,3},{3,2},{4,5},{5,4},{6,7},{7,6},{8,9},{9,8},{10,11... | collective-permute-start | bytes 786440 | tf_op jit(solution)/shard_map/ppermute | solution.py:419
  7.4 8.9 %collective-permute-start.1 = (f32[512,128]{1,0:T(8,128)S(1)}, f32[512,128]{1,0:T(8,128)S(1)}, u32[]{:S(2)}, u32[]{:S(2)}) collective-permute-start(f32[512,128]{1,0:T(8,128)S(1)} %get-tuple-element.32), channel_id=1, source_target_pairs={{0,255},{1,2},{2,1},{3,4},{4,3},{5,6},{6,5},{7,8},{8,7},{9,10},{10... | collective-permute-start | bytes 786440 | tf_op jit(solution)/shard_map/ppermute | solution.py:418
  18.3 32.9 %copy-start.3 = (f32[64]{0:T(128)S(1)}, f32[64]{0:T(128)}, u32[]{:S(2)}) copy-start(f32[64]{0:T(128)} %param.10) | copy-start | bytes 772
  18.3 1.3 %collective-permute-start.4 = (f32[104,128]{1,0:T(8,128)S(1)}, f32[104,128]{1,0:T(8,128)S(1)}, u32[]{:S(2)}, u32[]{:S(2)}) collective-permute-start(f32[104,128]{1,0:T(8,128)S(1)} %get-tuple-element.47), channel_id=1, source_target_pairs={{0,1},{1,0},{2,3},{3,2},{4,5},{5,4},{6,7},{7,6},{8,9},{9,8},{10,11... | collective-permute-start | bytes 159752 | tf_op jit(solution)/shard_map/ppermute | solution.py:431
  19.6 4.2 %collective-permute-start.5 = (f32[104,128]{1,0:T(8,128)S(1)}, f32[104,128]{1,0:T(8,128)S(1)}, u32[]{:S(2)}, u32[]{:S(2)}) collective-permute-start(f32[104,128]{1,0:T(8,128)S(1)} %add.21), channel_id=1, source_target_pairs={{0,2},{1,3},{2,0},{3,1},{4,6},{5,7},{6,4},{7,5},{8,10},{9,11},{10,... | collective-permute-start | bytes 159752 | tf_op jit(solution)/shard_map/ppermute | solution.py:448
  23.8 13.0 %collective-permute-start.6 = (f32[104,128]{1,0:T(8,128)S(1)}, f32[104,128]{1,0:T(8,128)S(1)}, u32[]{:S(2)}, u32[]{:S(2)}) collective-permute-start(f32[104,128]{1,0:T(8,128)S(1)} %add.22), channel_id=1, source_target_pairs={{0,6},{1,7},{2,4},{3,5},{4,2},{5,3},{6,0},{7,1},{8,14},{9,15},{10,... | collective-permute-start | bytes 159752 | tf_op jit(solution)/shard_map/ppermute | solution.py:448
  28.0 27.7 %collective-permute-start.2 = (f32[512,128]{1,0:T(8,128)S(1)}, f32[512,128]{1,0:T(8,128)S(1)}, u32[]{:S(2)}, u32[]{:S(2)}) collective-permute-start(f32[512,128]{1,0:T(8,128)S(1)} %get-tuple-element.39), channel_id=1, source_target_pairs={{0,1},{1,0},{2,3},{3,2},{4,5},{5,4},{6,7},{7,6},{8,9},{9,8},{10,11... | collective-permute-start | bytes 786440 | tf_op jit(solution)/shard_map/ppermute | solution.py:437
  28.1 27.7 %collective-permute-start.3 = (f32[512,128]{1,0:T(8,128)S(1)}, f32[512,128]{1,0:T(8,128)S(1)}, u32[]{:S(2)}, u32[]{:S(2)}) collective-permute-start(f32[512,128]{1,0:T(8,128)S(1)} %get-tuple-element.40), channel_id=1, source_target_pairs={{0,255},{1,2},{2,1},{3,4},{4,3},{5,6},{6,5},{7,8},{8,7},{9,10},{10... | collective-permute-start | bytes 786440 | tf_op jit(solution)/shard_map/ppermute | solution.py:436
  36.9 4.2 %collective-permute-start.7 = (f32[104,128]{1,0:T(8,128)S(1)}, f32[104,128]{1,0:T(8,128)S(1)}, u32[]{:S(2)}, u32[]{:S(2)}) collective-permute-start(f32[104,128]{1,0:T(8,128)S(1)} %add.23), channel_id=1, source_target_pairs={{0,64},{1,65},{2,66},{3,67},{4,68},{5,69},{6,70},{7,71},{8,72},{9,... | collective-permute-start | bytes 159752 | tf_op jit(solution)/shard_map/ppermute | solution.py:448
  41.1 5.4 %collective-permute-start.8 = (f32[104,128]{1,0:T(8,128)S(1)}, f32[104,128]{1,0:T(8,128)S(1)}, u32[]{:S(2)}, u32[]{:S(2)}) collective-permute-start(f32[104,128]{1,0:T(8,128)S(1)} %add.24), channel_id=1, source_target_pairs={{0,192},{1,193},{2,194},{3,195},{4,196},{5,197},{6,198},{7,199},{8... | collective-permute-start | bytes 159752 | tf_op jit(solution)/shard_map/ppermute | solution.py:448
  46.5 4.5 %collective-permute-start.9 = (f32[104,128]{1,0:T(8,128)S(1)}, f32[104,128]{1,0:T(8,128)S(1)}, u32[]{:S(2)}, u32[]{:S(2)}) collective-permute-start(f32[104,128]{1,0:T(8,128)S(1)} %add.25), channel_id=1, source_target_pairs={{0,8},{1,9},{2,10},{3,11},{4,12},{5,13},{6,14},{7,15},{8,0},{9,1},... | collective-permute-start | bytes 159752 | tf_op jit(solution)/shard_map/ppermute | solution.py:448
  51.0 4.6 %collective-permute-start.10 = (f32[104,128]{1,0:T(8,128)S(1)}, f32[104,128]{1,0:T(8,128)S(1)}, u32[]{:S(2)}, u32[]{:S(2)}) collective-permute-start(f32[104,128]{1,0:T(8,128)S(1)} %add.26), channel_id=1, source_target_pairs={{0,56},{1,57},{2,58},{3,59},{4,60},{5,61},{6,62},{7,63},{8,16},{9,... | collective-permute-start | bytes 159752 | tf_op jit(solution)/shard_map/ppermute | solution.py:448
  55.6 7.2 %collective-permute-start.11 = (f32[104,128]{1,0:T(8,128)S(1)}, f32[104,128]{1,0:T(8,128)S(1)}, u32[]{:S(2)}, u32[]{:S(2)}) collective-permute-start(f32[104,128]{1,0:T(8,128)S(1)} %add.27.mine), channel_id=1, source_target_pairs={{0,24},{1,25},{2,26},{3,27},{4,28},{5,29},{6,30},{7,31},{8,48},{9,... | collective-permute-start | bytes 159752 | tf_op jit(solution)/shard_map/ppermute | solution.py:451

commit v2 on v1

--- a/solution.py
+++ b/solution.py
@@ -7,6 +7,7 @@
 from jax.experimental.pallas import tpu as pltpu
 from jax.sharding import Mesh
 from jax.sharding import PartitionSpec as P
+
 
 C = 64
 BATCH = 2
@@ -18,6 +19,7 @@
 RIM = HB * PB
 EXT = BLK_DEV + 2 * HB
 MID = BLK_DEV - 2 * HB
+HALF = 3 * C // 4
 W2 = BATCH * C
 CHUNKS = PB * PB // 128
 AXES = ("patch_0", "patch_1", "patch_2", "strip")
@@ -44,7 +46,7 @@
 
 
 def slot_of(cols, b, j):
-    return jnp.bitwise_and(cols[b, j] - cols[0, 0] + HB, BLOCKS - 1)
+    return jnp.bitwise_and(cols[j, b] - cols[0, 0] + HB, BLOCKS - 1)
 
 
 def is_first_core(cols):
@@ -117,13 +119,15 @@
     cat[pl.ds(start, value.shape[0]), :] = jnp.concatenate([high, low], axis=1)
 
 
-def build(raw, fa_ref, at_ref):
+def build(raw, fa_ref, at_ref, block):
     low_lanes = lax.broadcasted_iota(jnp.int32, (CHUNKS, 128), 1) < PB
 
     def one(i, carry):
+        b = block(i)
+        group, rows = b // 8, pl.ds(b % 8, CHUNKS, stride=8)
         for pair in range(NB // 2):
-            even = raw[i, pl.ds(2 * pair, CHUNKS, stride=8), :]
-            odd = raw[i, pl.ds(2 * pair + 1, CHUNKS, stride=8), :]
+            even = raw[2 * pair, group, rows, :]
+            odd = raw[2 * pair + 1, group, rows, :]
             top = jnp.where(low_lanes, even, pltpu.roll(odd, PB, 1))
             bottom = jnp.where(low_lanes, pltpu.roll(even, PB, 1), odd)
             both = jnp.concatenate([top, bottom], axis=0)
@@ -132,28 +136,16 @@
             lanes = pl.ds(pair * 128, 128)
             stacked = jnp.concatenate([high, low], axis=0)
             fa_ref[i, :, lanes] = stacked
-            at_ref[i, lanes, :] = stacked.astype(F32).T.astype(BF16)
+            at_ref[i, lanes, :] = stacked.T
         return carry
 
     lax.fori_loop(0, MID, one, 0, unroll=4)
-
-
-def tile_copies(tiles, raw, sem, pieces):
-    return [
-        pltpu.make_async_copy(
-            tiles.at[pl.ds(start, count), :, pl.ds(k * 128, 128)],
-            raw.at[pl.ds(at, count), pl.ds(8 * k, NB), :],
-            sem.at[n * CHUNKS + k],
-        )
-        for n, (start, count, at) in enumerate(pieces)
-        for k in range(CHUNKS)
-    ]
 
 
 def rim_kernel(
     cols_hbm, tiles, g_hbm, x_hbm,
-    cols_ref, fa_ref, at_ref, acc, send_a, send_b,
-    cols, raw, g_rim, x_rim, sem, small,
+    cols_ref, raw, fa_ref, at_ref, acc, send_a, send_b,
+    cols, g_rim, x_rim, sem, small,
 ):
     to_cols = pltpu.make_async_copy(cols_hbm, cols, small.at[0])
     others = [pltpu.make_async_copy(cols_hbm, cols_ref, small.at[1])]
@@ -166,13 +158,21 @@
                 value.at[pl.ds(ROWS - RIM, RIM)], to.at[pl.ds(RIM, RIM)], small.at[3 + 2 * n]
             )
         )
-    copies = tile_copies(tiles, raw, sem, ((0, HB, 0), (BLK_DEV - HB, HB, HB)))
+    copies = [
+        pltpu.make_async_copy(
+            tiles.at[:, pl.ds(8 * group, 8), pl.ds(k * 128, 128)],
+            raw.at[:, group, pl.ds(8 * k, 8), :],
+            sem.at[group * CHUNKS + k],
+        )
+        for group in range(BLK_DEV // 8)
+        for k in range(CHUNKS)
+    ]
     for copy in copies + [to_cols] + others:
         copy.start()
     acc[...] = jnp.zeros_like(acc)
     for copy in copies:
         copy.wait()
-    build(raw, fa_ref, at_ref)
+    build(raw, fa_ref, at_ref, rim_block)
     to_cols.wait()
     for copy in others:
         copy.wait()
@@ -230,29 +230,19 @@
 
 
 def mid_kernel(
-    cols, tiles, g_ref, x_ref, acc_in, w_ref,
-    fa_ref, at_ref, first_ref, u_rim, part_ref, acc,
-    raw, cat, inner, u_mid, sem, *, scale,
+    cols, raw, g_ref, x_ref, acc_in,
+    fa_ref, at_ref, first_ref, u_mid, u_rim, part_ref,
+    cat, acc, *, scale,
 ):
-    copies = tile_copies(tiles, raw, sem, ((HB, MID, 0),))
-    for copy in copies:
-        copy.start()
     put_cat(cat, RIM, x_ref[...])
     acc[...] = acc_in[...]
-    for copy in copies:
-        copy.wait()
-    build(raw, fa_ref, at_ref)
+    build(raw, fa_ref, at_ref, mid_block)
     g_mid = g_ref.at[pl.ds(RIM, MID * PB)]
     spread(cols, at_ref, g_mid, acc, mid_block)
     u_mid[...] = acc[2 * RIM : 4 * RIM, :]
     u_rim[0:RIM, :] = acc[RIM : 2 * RIM, :]
     u_rim[RIM : 2 * RIM, :] = acc[4 * RIM : 5 * RIM, :]
     hop(cols, fa_ref, cat, first_ref, mid_block)
-    inner[...] = mixed(g_mid[...], both_maps(w_ref[1]).T) + 2.0 * mixed(
-        u_mid[...], both_maps(w_ref[2]).T
-    )
-    acc[...] = jnp.zeros_like(acc)
-    spread(cols, at_ref, inner, acc, mid_block)
     ((zero,),) = products([x_ref[...]], [g_ref[...]])
     ((one, two),) = products([first_ref[...]], [g_mid[...], u_mid[...]])
     part_ref[0 : C + C // 2, :] = scale * packed(zero, one, 2.0 * two - zero)
@@ -261,7 +251,7 @@
 
 
 def meet_kernel(
-    cols, fa_ref, x_ref, r_a, r_b, g_ref, u_part, part_ref, first_ref, u_ref, grads_ref, cat, *, scale
+    cols, fa_ref, x_ref, r_a, r_b, g_ref, u_part, part_ref, first_ref, u_ref, keep_ref, give_ref, cat, *, scale
 ):
     put_cat(cat, RIM, x_ref[...])
     for row, r in zip(rim_rows(cols), (r_a, r_b)):
@@ -271,18 +261,29 @@
     hop(cols, fa_ref, cat, first_ref, rim_block)
     g_rim = jnp.concatenate([g_ref[0:RIM, :], g_ref[ROWS - RIM :, :]], axis=0)
     ((one, two),) = products([first_ref[...]], [g_rim, u_ref[...]])
-    size = C + C // 2
-    grads_ref[0:size, :] = part_ref[0:size, :] + scale * packed(None, one, 2.0 * two)
-    grads_ref[size:, :] = part_ref[size:, :]
-
-
-def inner_kernel(
+    total = part_ref[0 : 2 * HALF, :] + scale * packed(None, one, 2.0 * two)
+    first = is_first_core(cols)
+    keep_ref[0:HALF, :] = jnp.where(first, total[:HALF], total[HALF:])
+    give_ref[0:HALF, :] = jnp.where(first, total[HALF:], total[:HALF])
+    keep_ref[HALF:, :] = part_ref[2 * HALF :, :]
+    give_ref[HALF:, :] = part_ref[2 * HALF :, :]
+
+
+def inner_rows(g, u, w_ref):
+    return mixed(g, both_maps(w_ref[1]).T) + 2.0 * mixed(u, both_maps(w_ref[2]).T)
+
+
+def inner_mid_kernel(cols, at_ref, g_ref, u_ref, w_ref, acc, inner):
+    inner[...] = inner_rows(g_ref[RIM : ROWS - RIM, :], u_ref[...], w_ref)
+    acc[...] = jnp.zeros_like(acc)
+    spread(cols, at_ref, inner, acc, mid_block)
+
+
+def inner_rim_kernel(
     cols, at_ref, g_ref, u_ref, w_ref, first_ref, acc_in, u2_ref, send_a, send_b, inner, acc
 ):
     g_rim = jnp.concatenate([g_ref[0:RIM, :], g_ref[ROWS - RIM :, :]], axis=0)
-    inner[...] = mixed(g_rim, both_maps(w_ref[1]).T) + 2.0 * mixed(
-        u_ref[...], both_maps(w_ref[2]).T
-    )
+    inner[...] = inner_rows(g_rim, u_ref[...], w_ref)
     acc[...] = acc_in[...]
     spread(cols, at_ref, inner, acc, rim_block)
     u2_ref[...] = acc[RIM : RIM + ROWS, :]
@@ -339,20 +340,23 @@
         back_ref[own, :] = back_ref[own, :] + r[RIM : 2 * RIM, :]
 
 
-def final_kernel(mine, theirs, weight_ref, bias_ref):
-    total = mine[...] + theirs[...]
-    half = C // 2
-    weight_ref[0] = total[:C, :C]
-    weight_ref[1] = pltpu.roll(total[:C], C, 1)[:, :C]
-    weight_ref[2, 0:half, :] = total[C : C + half, :C]
-    weight_ref[2, half:C, :] = pltpu.roll(total[C : C + half], C, 1)[:, :C]
-    bias_ref[...] = total[C + half : C + half + 1, :C]
-
-
-def call(kernel, name, out, specs, scratch, flops, moved):
+def final_kernel(cols, mine, theirs, weight_ref, bias_ref):
+    first = is_first_core(cols)
+    top = jnp.where(first, mine[...], theirs[...])
+    bottom = jnp.where(first, theirs[...], mine[...])
+    rest = C - HALF
+    for k, (upper, lower) in enumerate(
+        ((top, bottom), (pltpu.roll(top, C, 1), pltpu.roll(bottom, C, 1)))
+    ):
+        weight_ref[k, 0:HALF, :] = upper[:HALF, :C]
+        weight_ref[k, HALF:C, :] = lower[:rest, :C]
+        weight_ref[2, k * (C // 2) : (k + 1) * (C // 2), :] = lower[rest:HALF, :C]
+    bias_ref[...] = top[HALF : HALF + 1, :C]
+
+
+def call(kernel, out, specs, scratch, flops, moved):
     return pl.pallas_call(
         kernel,
-        name=name,
         out_shape=[jax.ShapeDtypeStruct(s, d) for s, d in out],
         in_specs=specs,
         out_specs=[VMEM] * len(out),
@@ -374,18 +378,36 @@
 IN_CHIP = [(i, i ^ 1) for i in range(COUNT)]
 CROSS = [(i, (i + 1) % COUNT) if i % 2 else (i, (i - 1) % COUNT) for i in range(COUNT)]
 RING4 = ((1, 0, 3, 2), (3, 2, 1, 0))
-RING8 = ((1, 0, 3, 2, 5, 4, 7, 6), (7, 2, 1, 4, 3, 6, 5, 0), (3, 6, 5, 0, 7, 2, 1, 4))
-
-
-def moves():
-    steps = [IN_CHIP]
-    for table in RING4:
-        steps.append([(i, index(a, b, table[c], s)) for i, (a, b, c, s) in enumerate(map(place, range(COUNT)))])
-    for table in RING4:
-        steps.append([(i, index(table[a], b, c, s)) for i, (a, b, c, s) in enumerate(map(place, range(COUNT)))])
-    for table in RING8:
-        steps.append([(i, index(a, table[b], c, s)) for i, (a, b, c, s) in enumerate(map(place, range(COUNT)))])
-    return steps
+PAIRS = (1, 0, 3, 2, 5, 4, 7, 6)
+FAR = (5, 4, 7, 6, 1, 0, 3, 2)
+NEXT = (6, 3, 0, 5, 2, 7, 4, 1)
+NEAR = (7, 2, 1, 4, 3, 6, 5, 0)
+
+
+def along(axis, table):
+    pairs = []
+    for i in range(COUNT):
+        at = list(place(i))
+        at[axis] = table[at[axis]]
+        pairs.append((i, index(*at)))
+    return pairs
+
+
+def sent(value, pairs):
+    return lax.ppermute(value, AXES, pairs)
+
+
+def by_pair(own, near, following, far):
+    z = lax.axis_index("patch_1")
+    q, step = z // 2, 2 * (z % 2) - 1
+    at = [jnp.bitwise_and(q + offset, 3) for offset in (0, step, -step, 2)]
+    terms = []
+    for k in range(4):
+        term = far
+        for place_of, value in zip(at[:3], (own, near, following)):
+            term = jnp.where(place_of == k, value, term)
+        terms.append(term)
+    return (terms[0] + terms[1]) + (terms[2] + terms[3])
 
 
 def shards(features, lap_tiles, columns, weights, bias_term, cotangent):
@@ -393,10 +415,11 @@
     field = ((ROWS, W2), F32)
     half = ((ROWS // 2, W2), F32)
     extended = ((EXT * PB, W2), F32)
-    sums = ((C + C // 2 + 8, W2), F32)
+    sums = ((2 * HALF + 8, W2), F32)
+    share = ((HALF + 8, W2), F32)
     natural = ((MID, 2 * PB, NB * PB), BF16)
     turned = ((MID, NB * PB, 2 * PB), BF16)
-    raw = pltpu.VMEM((MID, CHUNKS * 8, 128), F32)
+    raw = ((NB, BLK_DEV // 8, CHUNKS * 8, 128), F32)
     cat = pltpu.VMEM((EXT * PB, 2 * W2), BF16)
     half_scratch = pltpu.VMEM((ROWS // 2, W2), F32)
 
@@ -406,55 +429,71 @@
 
         return body
 
-    cols, fa_rim, at_rim, acc, s_a, s_b = call(
-        rim_kernel, "rim", [((BLK_DEV, NB), jnp.int32), natural, turned, extended, half, half],
+    in_hbm = [
+        pltpu.with_memory_space_constraint(value, pltpu.HBM)
+        for value in (columns.T, jnp.transpose(lap_tiles, (1, 0, 2)), cotangent, features)
+    ]
+    cols, raw, fa_rim, at_rim, acc, s_a, s_b = call(
+        rim_kernel,
+        [((NB, BLK_DEV), jnp.int32), raw, natural, turned, extended, half, half],
         [HBM] * 4,
         [
-            pltpu.SMEM((BLK_DEV, NB), jnp.int32), raw, half_scratch, half_scratch,
+            pltpu.SMEM((NB, BLK_DEV), jnp.int32), half_scratch, half_scratch,
             pltpu.SemaphoreType.DMA((2 * CHUNKS,)), pltpu.SemaphoreType.DMA((6,)),
         ],
         400_000_000, 4_000_000,
-    )(columns, lap_tiles, cotangent, features)
-    r_b = lax.ppermute(s_b, AXES, CROSS)
-    r_a = lax.ppermute(s_a, AXES, IN_CHIP)
-    fa_mid, at_mid, f_mid, u_rim, part, acc = call(
-        scaled(mid_kernel), "mid", [natural, turned, half, half, sums, extended],
-        [SMEM, HBM] + [VMEM] * 4,
-        [raw, cat, half_scratch, half_scratch, pltpu.SemaphoreType.DMA((CHUNKS,))],
-        1_600_000_000, 9_000_000,
-    )(cols, lap_tiles, cotangent, features, acc, weights)
-    f_rim, u_rim, grads = call(
-        scaled(meet_kernel), "meet", [half, half, sums], [SMEM] + [VMEM] * 7, [cat],
+    )(*in_hbm)
+    r_b = sent(s_b, CROSS)
+    r_a = sent(s_a, IN_CHIP)
+    fa_mid, at_mid, f_mid, u_mid, u_rim, part = call(
+        scaled(mid_kernel), [natural, turned, half, half, half, sums],
+        [SMEM] + [VMEM] * 4, [cat, pltpu.VMEM(*extended)], 1_600_000_000, 9_000_000,
+    )(cols, raw, cotangent, features, acc)
+    f_rim, u_rim, keep, give = call(
+        scaled(meet_kernel), [half, half, share, share], [SMEM] + [VMEM] * 7, [cat],
         400_000_000, 3_000_000,
     )(cols, fa_rim, features, r_a, r_b, cotangent, u_rim, part)
-    steps = moves()
-    grads = grads + lax.ppermute(grads, AXES, steps[0])
+    grads = keep + sent(give, IN_CHIP)
+    (acc,) = call(
+        inner_mid_kernel, [extended], [SMEM] + [VMEM] * 4, [half_scratch],
+        400_000_000, 3_000_000,
+    )(cols, at_mid, cotangent, u_mid, weights)
     u2, s_a, s_b = call(
-        inner_kernel, "inner", [field, half, half], [SMEM] + [VMEM] * 6,
+        inner_rim_kernel, [field, half, half], [SMEM] + [VMEM] * 6,
         [half_scratch, pltpu.VMEM(*extended)], 400_000_000, 3_000_000,
     )(cols, at_rim, cotangent, u_rim, weights, f_rim, acc)
-    s_b = lax.ppermute(s_b, AXES, CROSS)
-    s_a = lax.ppermute(s_a, AXES, IN_CHIP)
+    s_b = sent(s_b, CROSS)
+    s_a = sent(s_a, IN_CHIP)
     bias_row = bias_term.reshape(1, C)
     o_mid, b_mid = call(
-        last_mid_kernel, "last_mid", [half, half], [SMEM] + [VMEM] * 8, [cat, half_scratch],
+        last_mid_kernel, [half, half], [SMEM] + [VMEM] * 8, [cat, half_scratch],
         600_000_000, 4_000_000,
     )(cols, fa_mid, features, cotangent, f_mid, f_rim, u2, weights, bias_row)
     output, input_grad = call(
-        last_rim_kernel, "last_rim", [field, field], [SMEM] + [VMEM] * 12, [cat, half_scratch],
+        last_rim_kernel, [field, field], [SMEM] + [VMEM] * 12, [cat, half_scratch],
         600_000_000, 5_000_000,
     )(cols, fa_rim, features, cotangent, f_mid, f_rim, s_a, s_b, u2, weights, bias_row, o_mid, b_mid)
-    for step in steps[1:-1]:
-        grads = grads + lax.ppermute(grads, AXES, step)
+    grads = grads + sent(grads, along(2, RING4[0]))
+    grads = grads + sent(grads, along(2, RING4[1]))
+    grads = grads + sent(grads, along(0, RING4[0]))
+    grads = grads + sent(grads, along(0, RING4[1]))
+    grads = grads + sent(grads, along(1, PAIRS))
+    far = sent(grads, along(1, FAR))
+    following = sent(grads, along(1, NEXT))
+    near = sent(grads, along(1, NEAR))
+    grads = by_pair(grads, near, following, far)
+    theirs = sent(grads, IN_CHIP)
     weight_grad, bias_grad = call(
-        final_kernel, "final", [((3, C, C), F32), ((1, C), F32)], [VMEM, VMEM], [], 1000, 100_000
-    )(grads, lax.ppermute(grads, AXES, steps[-1]))
+        final_kernel, [((3, C, C), F32), ((1, C), F32)], [SMEM, VMEM, VMEM], [],
+        1000, 100_000,
+    )(cols, grads, theirs)
     return output, input_grad, weight_grad, bias_grad.reshape(C)
 
 
 def solution(mesh):
     grid = Mesh(mesh.devices.reshape(*SHAPE), AXES)
     placed = (P(AXES, None), P(AXES, None, None), P(AXES, None), P(), P(), P(AXES, None))
+
     return jax.shard_map(
         shards,
         mesh=grid,

time: 63.7 us -> 68 us (1.068)
  the two profiles are of different devices: /device:TPU:32 before, /device:TPU:1 now
where the time goes in v2:
time: 68 us; the launch traced here: 67.7 us
  starting transfers between devices  28.2 us (41%)
  Pallas kernels  19.5 us (29%)
  waiting for transfers between devices  14.8 us (22%)
  local copies, waits for them, and re-layouts  3.68 us (5%)
  between operations  0.82 us (1%)
  other arithmetic  0.81 us (1%)
    ppermute x14, starting transfers between devices, sent(): return lax.ppermute(value, AXES, pairs)  28.2 us
    ppermute x14, waiting for transfers between devices, sent(): return lax.ppermute(value, AXES, pairs)  14.8 us
    pallas_call x1, Pallas kernels, shards(): call(rim_kernel, [((NB, BLK_DEV), jnp.int32), raw, natural, turned, exten...  4.07 us
    pallas_call x1, Pallas kernels, shards(): call(scaled(mid_kernel), [natural, turned, half, half, half, sums], [SMEM...  3.78 us
    unnamed x20, local copies, waits for them, and re-layouts  3.68 us
    pallas_call x1, Pallas kernels, shards(): call(last_rim_kernel, [field, field], [SMEM] + [VMEM] * 12, [cat, half_sc...  2.92 us
    pallas_call x1, Pallas kernels, shards(): call(inner_rim_kernel, [field, half, half], [SMEM] + [VMEM] * 6, [half_sc...  1.93 us
    pallas_call x1, Pallas kernels, shards(): call(inner_mid_kernel, [extended], [SMEM] + [VMEM] * 4, [half_scratch], 4...  1.86 us
  transfers between devices with their start and end apart: 14, of which 6 were waited for; matrix products, arithmetic and copies ran while one was open for 0% of the time, Pallas kernels for 16%

profile of v2, /device:TPU:1, one launch (start us, length us, event | category | flops | bytes accessed | tf_op | source)
XLA Modules:
  0.0 67.7 jit_solution(4980402944372595553)
XLA Ops:
  0.7 4.1 %shard_map.93 = (s32[6,16]{1,0:T(8,128)S(1)}, f32[6,2,256,128]{3,2,1,0:T(8,128)S(1)}, bf16[8,128,384]{2,1,0:T(8,128)(2,1)S(1)}, bf16[8,384,128]{2,1,0:T(8,128)(2...) custom-call(s32[6,16]{1,0:T(8,128)} %bitcast.7, f32[6,16,4096]{2,1,0:T(8,128)} %bitcast.6, ...), custom_call_target="tpu_custom_call" | custom-call | flops 400000000 | bytes 4000000 | tf_op jit(solution)/shard_map/pallas_call | solution.py:436
  4.7 0.9 %copy-done.3 = bf16[8,384,128]{2,1,0:T(8,128)(2,1)} copy-done((bf16[8,384,128]{2,1,0:T(8,128)(2,1)}, bf16[8,384,128]{2,1,0:T(8,128)(2,1)S(1)}, u32[]{:S(2)}) %copy-start.3) | copy-done | bytes 786456
  5.6 3.2 %collective-permute-start = (f32[512,128]{1,0:T(8,128)S(1)}, f32[512,128]{1,0:T(8,128)S(1)}, u32[]{:S(2)}, u32[]{:S(2)}) collective-permute-start(f32[512,128]{1,0:T(8,128)S(1)} %get-tuple-element.35), channel_id=1, source_target_pairs={{0,1},{1,0},{2,3},{3,2},{4,5},{5,4},{6,7},{7,6},{8,9},{9,8},{10,11... | collective-permute-start | bytes 786440 | tf_op jit(solution)/shard_map/ppermute | solution.py:397
  8.8 0.0 collective-permute-start.1
  8.9 3.8 %shard_map.94 = (bf16[8,128,384]{2,1,0:T(8,128)(2,1)S(1)}, bf16[8,384,128]{2,1,0:T(8,128)(2,1)S(1)}, f32[512,128]{1,0:T(8,128)S(1)}, f32[512,128]{1,0:T(8,128)S(...) custom-call(s32[6,16]{1,0:T(8,128)S(1)} %get-tuple-element.30.refs_0_.cols, ...), custom_call_target="tpu_custom_call" | custom-call | flops 1600000000 | bytes 9000000 | tf_op jit(solution)/shard_map/pallas_call | solution.py:448
  12.6 0.9 %copy-done.5 = bf16[8,384,128]{2,1,0:T(8,128)(2,1)} copy-done((bf16[8,384,128]{2,1,0:T(8,128)(2,1)}, bf16[8,384,128]{2,1,0:T(8,128)(2,1)S(1)}, u32[]{:S(2)}) %copy-start.5) | copy-done | bytes 786456
  13.6 1.1 %collective-permute-done.1.refs_4_ = f32[512,128]{1,0:T(8,128)S(1)} collective-permute-done((f32[512,128]{1,0:T(8,128)S(1)}, f32[512,128]{1,0:T(8,128)S(1)}, u32[]{:S(2)}, u32[]{:S(2)}) %collective-permute-start.1) | collective-permute-done | bytes 262176 | tf_op jit(solution)/shard_map/ppermute | solution.py:397
  14.6 1.8 %shard_map.95 = (f32[512,128]{1,0:T(8,128)S(1)}, f32[512,128]{1,0:T(8,128)S(1)}, f32[56,128]{1,0:T(8,128)S(1)}, f32[56,128]{1,0:T(8,128)S(1)}) custom-call(s32[6,16]{1,0:T(8,128)S(1)} %get-tuple-element.30.refs_0_.cols, bf16[8,128,384]{2,1,0:T(8,128)(2,1)S(1)} %get-tuple-element.31.refs_1_.fa_ref, f32[1024,128]{1,0:T(8,128)S(1)} %copy-done.1, ...), custom_call_target="tpu_custom_call" | custom-call | flops 400000000 | bytes 3000000 | tf_op jit(solution)/shard_map/pallas_call | solution.py:452
  16.5 0.0 copy-start.7
  16.5 0.7 %copy-done.7 = f32[512,128]{1,0:T(8,128)} copy-done((f32[512,128]{1,0:T(8,128)}, f32[512,128]{1,0:T(8,128)S(1)}, u32[]{:S(2)}) %copy-start.7) | copy-done | bytes 262168
  17.2 7.9 %collective-permute-start.4 = (f32[56,128]{1,0:T(8,128)S(1)}, f32[56,128]{1,0:T(8,128)S(1)}, u32[]{:S(2)}, u32[]{:S(2)}) collective-permute-start(f32[56,128]{1,0:T(8,128)S(1)} %get-tuple-element.53), channel_id=1, source_target_pairs={{0,1},{1,0},{2,3},{3,2},{4,5},{5,4},{6,7},{7,6},{8,9},{9,8},{10,11... | collective-permute-start | bytes 86024 | tf_op jit(solution)/shard_map/ppermute | solution.py:397
  25.0 0.9 %collective-permute-done.4 = f32[56,128]{1,0:T(8,128)S(1)} collective-permute-done((f32[56,128]{1,0:T(8,128)S(1)}, f32[56,128]{1,0:T(8,128)S(1)}, u32[]{:S(2)}, u32[]{:S(2)}) %collective-permute-start.4) | collective-permute-done | bytes 28704 | tf_op jit(solution)/shard_map/ppermute | solution.py:397
  25.9 0.0 collective-permute-start.5
  25.9 2.7 %collective-permute-done.5 = f32[56,128]{1,0:T(8,128)S(1)} collective-permute-done((f32[56,128]{1,0:T(8,128)S(1)}, f32[56,128]{1,0:T(8,128)S(1)}, u32[]{:S(2)}, u32[]{:S(2)}) %collective-permute-start.5) | collective-permute-done | bytes 28704 | tf_op jit(solution)/shard_map/ppermute | solution.py:397
  28.6 3.9 %collective-permute-done.6 = f32[56,128]{1,0:T(8,128)S(1)} collective-permute-done((f32[56,128]{1,0:T(8,128)S(1)}, f32[56,128]{1,0:T(8,128)S(1)}, u32[]{:S(2)}, u32[]{:S(2)}) %collective-permute-start.6) | collective-permute-done | bytes 28704 | tf_op jit(solution)/shard_map/ppermute | solution.py:397
  32.6 2.7 %collective-permute-done.7 = f32[56,128]{1,0:T(8,128)S(1)} collective-permute-done((f32[56,128]{1,0:T(8,128)S(1)}, f32[56,128]{1,0:T(8,128)S(1)}, u32[]{:S(2)}, u32[]{:S(2)}) %collective-permute-start.7) | collective-permute-done | bytes 28704 | tf_op jit(solution)/shard_map/ppermute | solution.py:397
  35.3 0.5 collective-permute-start.8
  35.8 3.5 %collective-permute-done.8 = f32[56,128]{1,0:T(8,128)} collective-permute-done((f32[56,128]{1,0:T(8,128)S(1)}, f32[56,128]{1,0:T(8,128)}, u32[]{:S(2)}, u32[]{:S(2)}) %collective-permute-start.8) | collective-permute-done | bytes 28704 | tf_op jit(solution)/shard_map/ppermute | solution.py:397
  39.3 0.8 %add.45 = f32[56,128]{1,0:T(8,128)S(1)} add(f32[56,128]{1,0:T(8,128)S(1)} %add.44, f32[56,128]{1,0:T(8,128)} %collective-permute-done.8) | non-fusion elementwise | flops 7168 | bytes 86016 | tf_op jit(solution)/shard_map/add | solution.py:479
  40.1 0.0 collective-permute-start.9
  40.1 1.1 %copy-done.6 = bf16[8,384,128]{2,1,0:T(8,128)(2,1)S(1)} copy-done((bf16[8,384,128]{2,1,0:T(8,128)(2,1)S(1)}, bf16[8,384,128]{2,1,0:T(8,128)(2,1)}, u32[]{:S(2)}) %copy-start.6) | copy-done | bytes 786456
  41.2 1.9 %shard_map.96.acc_in = f32[1536,128]{1,0:T(8,128)S(1)} custom-call(s32[6,16]{1,0:T(8,128)S(1)} %get-tuple-element.30.refs_0_.cols, bf16[8,384,128]{2,1,0:T(8,128)(2,1)S(1)} %copy-done.6, f32[1024,128]{1,0:T(8,128)S(1)} %copy-done, f32[512,128]{1,0:T(8,128)S(1)} %get-tuple-element.43.u_ref, f32[3,64,64]{2,1,0:T(8,128)S(1)} %copy-done.2), custom_call_target="tpu_custom_call" | custom-call | flops 400000000 | bytes 3000000 | tf_op jit(solution)/shard_map/pallas_call | solution.py:457
  43.1 0.0 copy-start.9
  43.1 2.9 %collective-permute-start.10 = (f32[56,128]{1,0:T(8,128)S(1)}, f32[56,128]{1,0:T(8,128)S(1)}, u32[]{:S(2)}, u32[]{:S(2)}) collective-permute-start(f32[56,128]{1,0:T(8,128)S(1)} %add.46), channel_id=1, source_target_pairs={{0,48},{1,49},{2,50},{3,51},{4,52},{5,53},{6,54},{7,55},{8,24},{9,... | collective-permute-start | bytes 86024 | tf_op jit(solution)/shard_map/ppermute | solution.py:397
  46.0 1.0 %collective-permute-start.11 = (f32[56,128]{1,0:T(8,128)S(1)}, f32[56,128]{1,0:T(8,128)S(1)}, u32[]{:S(2)}, u32[]{:S(2)}) collective-permute-start(f32[56,128]{1,0:T(8,128)S(1)} %add.46), channel_id=1, source_target_pairs={{0,56},{1,57},{2,58},{3,59},{4,60},{5,61},{6,62},{7,63},{8,16},{9,... | collective-permute-start | bytes 86024 | tf_op jit(solution)/shard_map/ppermute | solution.py:397
  47.1 0.3 collective-permute-start.12
  47.3 1.9 %shard_map.97 = (f32[1024,128]{1,0:T(8,128)S(1)}, f32[512,128]{1,0:T(8,128)S(1)}, f32[512,128]{1,0:T(8,128)S(1)}) custom-call(s32[6,16]{1,0:T(8,128)S(1)} %get-tuple-element.30.refs_0_.cols, bf16[8,384,128]{2,1,0:T(8,128)(2,1)S(1)} %copy-done.4, f32[1024,128]{1,0:T(8,128)S(1)} %copy-done, f32[512,128]{1,0:T(8,128)S(1)} %copy-done.8, ...), custom_call_target="tpu_custom_call" | custom-call | flops 400000000 | bytes 3000000 | tf_op jit(solution)/shard_map/pallas_call | solution.py:461
  49.3 5.6 %collective-permute-start.2 = (f32[512,128]{1,0:T(8,128)S(1)}, f32[512,128]{1,0:T(8,128)S(1)}, u32[]{:S(2)}, u32[]{:S(2)}) collective-permute-start(f32[512,128]{1,0:T(8,128)S(1)} %get-tuple-element.44), channel_id=1, source_target_pairs={{0,1},{1,0},{2,3},{3,2},{4,5},{5,4},{6,7},{7,6},{8,9},{9,8},{10,11... | collective-permute-start | bytes 786440 | tf_op jit(solution)/shard_map/ppermute | solution.py:397
  54.9 6.7 %collective-permute-start.13 = (f32[56,128]{1,0:T(8,128)S(1)}, f32[56,128]{1,0:T(8,128)S(1)}, u32[]{:S(2)}, u32[]{:S(2)}) collective-permute-start(f32[56,128]{1,0:T(8,128)S(1)} %add_add_fusion.mine), channel_id=1, source_target_pairs={{0,1},{1,0},{2,3},{3,2},{4,5},{5,4},{6,7},{7,6},{8,9},{9,8},{10,11... | collective-permute-start | bytes 86024 | tf_op jit(solution)/shard_map/ppermute | solution.py:397
  61.7 1.8 %shard_map.98 = (f32[512,128]{1,0:T(8,128)S(1)}, f32[512,128]{1,0:T(8,128)S(1)}) custom-call(s32[6,16]{1,0:T(8,128)S(1)} %get-tuple-element.30.refs_0_.cols, bf16[8,128,384]{2,1,0:T(8,128)(2,1)S(1)} %get-tuple-element.47.fa_ref, f32[1024,128]{1,0:T(8,128)S(1)} %copy-done.1, f32[1024,128]{1,0:T(8,128)S(1)} %copy-done, ...), custom_call_target="tpu_custom_call" | custom-call | flops 600000000 | bytes 4000000 | tf_op jit(solution)/shard_map/pallas_call | solution.py:468
  63.5 1.3 %shard_map.100 = (f32[3,64,64]{2,1,0:T(8,128)}, f32[1,64]{1,0:T(1,128)}) custom-call(s32[6,16]{1,0:T(8,128)S(1)} %get-tuple-element.30.refs_0_.cols, f32[56,128]{1,0:T(8,128)S(1)} %add_add_fusion.mine, f32[56,128]{1,0:T(8,128)S(1)} %collective-permute-done.13.theirs), custom_call_target="tpu_custom_call" | custom-call | flops 1000 | bytes 100000 | tf_op jit(solution)/shard_map/pallas_call | solution.py:486
  64.8 2.9 %shard_map.99 = (f32[1024,128]{1,0:T(8,128)}, f32[1024,128]{1,0:T(8,128)}) custom-call(s32[6,16]{1,0:T(8,128)S(1)} %get-tuple-element.30.refs_0_.cols, bf16[8,128,384]{2,1,0:T(8,128)(2,1)S(1)} %get-tuple-element.31.refs_1_.fa_ref, f32[1024,128]{1,0:T(8,128)S(1)} %copy-done.1, f32[1024,128]{1,0:T(8,128)S(1)} %copy-done, ...), custom_call_target="tpu_custom_call" | custom-call | flops 600000000 | bytes 5000000 | tf_op jit(solution)/shard_map/pallas_call | solution.py:472
  (31 shorter events, 0.1 us)
Async XLA Ops:
  0.6 8.2 %copy-start = (f32[1024,128]{1,0:T(8,128)S(1)}, f32[1024,128]{1,0:T(8,128)}, u32[]{:S(2)}) copy-start(f32[1024,128]{1,0:T(8,128)} %g_ref.7) | copy-start | bytes 1572868
  0.6 8.2 %copy-start.1 = (f32[1024,128]{1,0:T(8,128)S(1)}, f32[1024,128]{1,0:T(8,128)}, u32[]{:S(2)}) copy-start(f32[1024,128]{1,0:T(8,128)} %x_ref.3) | copy-start | bytes 1572868
  4.7 0.9 %copy-start.3 = (bf16[8,384,128]{2,1,0:T(8,128)(2,1)}, bf16[8,384,128]{2,1,0:T(8,128)(2,1)S(1)}, u32[]{:S(2)}) copy-start(bf16[8,384,128]{2,1,0:T(8,128)(2,1)S(1)} %get-tuple-element.40.at_ref) | copy-start | bytes 2359300
  5.6 7.9 %collective-permute-start = (f32[512,128]{1,0:T(8,128)S(1)}, f32[512,128]{1,0:T(8,128)S(1)}, u32[]{:S(2)}, u32[]{:S(2)}) collective-permute-start(f32[512,128]{1,0:T(8,128)S(1)} %get-tuple-element.35), channel_id=1, source_target_pairs={{0,1},{1,0},{2,3},{3,2},{4,5},{5,4},{6,7},{7,6},{8,9},{9,8},{10,11... | collective-permute-start | bytes 786440 | tf_op jit(solution)/shard_map/ppermute | solution.py:397
  8.8 5.8 %collective-permute-start.1 = (f32[512,128]{1,0:T(8,128)S(1)}, f32[512,128]{1,0:T(8,128)S(1)}, u32[]{:S(2)}, u32[]{:S(2)}) collective-permute-start(f32[512,128]{1,0:T(8,128)S(1)} %get-tuple-element.36), channel_id=1, source_target_pairs={{0,255},{1,2},{2,1},{3,4},{4,3},{5,6},{6,5},{7,8},{8,7},{9,10},{10... | collective-permute-start | bytes 786440 | tf_op jit(solution)/shard_map/ppermute | solution.py:397
  12.6 0.9 %copy-start.5 = (bf16[8,384,128]{2,1,0:T(8,128)(2,1)}, bf16[8,384,128]{2,1,0:T(8,128)(2,1)S(1)}, u32[]{:S(2)}) copy-start(bf16[8,384,128]{2,1,0:T(8,128)(2,1)S(1)} %get-tuple-element.42.at_ref) | copy-start | bytes 2359300
  14.6 25.4 %copy-start.2 = (f32[3,64,64]{2,1,0:T(8,128)S(1)}, f32[3,64,64]{2,1,0:T(8,128)}, u32[]{:S(2)}) copy-start(f32[3,64,64]{2,1,0:T(8,128)} %w_ref.7) | copy-start | bytes 147460
  16.5 0.7 %copy-start.7 = (f32[512,128]{1,0:T(8,128)}, f32[512,128]{1,0:T(8,128)S(1)}, u32[]{:S(2)}) copy-start(f32[512,128]{1,0:T(8,128)S(1)} %get-tuple-element.41.u_ref) | copy-start | bytes 786436
  17.2 8.7 %collective-permute-start.4 = (f32[56,128]{1,0:T(8,128)S(1)}, f32[56,128]{1,0:T(8,128)S(1)}, u32[]{:S(2)}, u32[]{:S(2)}) collective-permute-start(f32[56,128]{1,0:T(8,128)S(1)} %get-tuple-element.53), channel_id=1, source_target_pairs={{0,1},{1,0},{2,3},{3,2},{4,5},{5,4},{6,7},{7,6},{8,9},{9,8},{10,11... | collective-permute-start | bytes 86024 | tf_op jit(solution)/shard_map/ppermute | solution.py:397
  25.9 2.7 %collective-permute-start.5 = (f32[56,128]{1,0:T(8,128)S(1)}, f32[56,128]{1,0:T(8,128)S(1)}, u32[]{:S(2)}, u32[]{:S(2)}) collective-permute-start(f32[56,128]{1,0:T(8,128)S(1)} %add.41), channel_id=1, source_target_pairs={{0,2},{1,3},{2,0},{3,1},{4,6},{5,7},{6,4},{7,5},{8,10},{9,11},{10,... | collective-permute-start | bytes 86024 | tf_op jit(solution)/shard_map/ppermute | solution.py:397
  28.6 3.9 %collective-permute-start.6 = (f32[56,128]{1,0:T(8,128)S(1)}, f32[56,128]{1,0:T(8,128)S(1)}, u32[]{:S(2)}, u32[]{:S(2)}) collective-permute-start(f32[56,128]{1,0:T(8,128)S(1)} %add.42), channel_id=1, source_target_pairs={{0,6},{1,7},{2,4},{3,5},{4,2},{5,3},{6,0},{7,1},{8,14},{9,15},{10,... | collective-permute-start | bytes 86024 | tf_op jit(solution)/shard_map/ppermute | solution.py:397
  32.6 2.7 %collective-permute-start.7 = (f32[56,128]{1,0:T(8,128)S(1)}, f32[56,128]{1,0:T(8,128)S(1)}, u32[]{:S(2)}, u32[]{:S(2)}) collective-permute-start(f32[56,128]{1,0:T(8,128)S(1)} %add.43), channel_id=1, source_target_pairs={{0,64},{1,65},{2,66},{3,67},{4,68},{5,69},{6,70},{7,71},{8,72},{9,... | collective-permute-start | bytes 86024 | tf_op jit(solution)/shard_map/ppermute | solution.py:397
  35.3 4.0 %collective-permute-start.8 = (f32[56,128]{1,0:T(8,128)S(1)}, f32[56,128]{1,0:T(8,128)}, u32[]{:S(2)}, u32[]{:S(2)}) collective-permute-start(f32[56,128]{1,0:T(8,128)S(1)} %add.44), channel_id=1, source_target_pairs={{0,192},{1,193},{2,194},{3,195},{4,196},{5,197},{6,198},{7,199},{8... | collective-permute-start | bytes 86024 | tf_op jit(solution)/shard_map/ppermute | solution.py:397
  35.8 11.5 %copy-start.4 = (bf16[8,384,128]{2,1,0:T(8,128)(2,1)S(1)}, bf16[8,384,128]{2,1,0:T(8,128)(2,1)}, u32[]{:S(2)}) copy-start(bf16[8,384,128]{2,1,0:T(8,128)(2,1)} %copy-done.3) | copy-start | bytes 2359300
  40.1 3.0 %collective-permute-start.9 = (f32[56,128]{1,0:T(8,128)S(1)}, f32[56,128]{1,0:T(8,128)S(1)}, u32[]{:S(2)}, u32[]{:S(2)}) collective-permute-start(f32[56,128]{1,0:T(8,128)S(1)} %add.45), channel_id=1, source_target_pairs={{0,8},{1,9},{2,10},{3,11},{4,12},{5,13},{6,14},{7,15},{8,0},{9,1},... | collective-permute-start | bytes 86024 | tf_op jit(solution)/shard_map/ppermute | solution.py:397
  40.1 1.1 %copy-start.6 = (bf16[8,384,128]{2,1,0:T(8,128)(2,1)S(1)}, bf16[8,384,128]{2,1,0:T(8,128)(2,1)}, u32[]{:S(2)}) copy-start(bf16[8,384,128]{2,1,0:T(8,128)(2,1)} %copy-done.5) | copy-start | bytes 2359300
  41.2 6.1 %copy-start.8 = (f32[512,128]{1,0:T(8,128)S(1)}, f32[512,128]{1,0:T(8,128)}, u32[]{:S(2)}) copy-start(f32[512,128]{1,0:T(8,128)} %copy-done.7) | copy-start | bytes 786436
  43.1 18.6 %copy-start.9 = (f32[64]{0:T(128)S(1)}, f32[64]{0:T(128)}, u32[]{:S(2)}) copy-start(f32[64]{0:T(128)} %param.10) | copy-start | bytes 772
  43.1 11.8 %collective-permute-start.10 = (f32[56,128]{1,0:T(8,128)S(1)}, f32[56,128]{1,0:T(8,128)S(1)}, u32[]{:S(2)}, u32[]{:S(2)}) collective-permute-start(f32[56,128]{1,0:T(8,128)S(1)} %add.46), channel_id=1, source_target_pairs={{0,48},{1,49},{2,50},{3,51},{4,52},{5,53},{6,54},{7,55},{8,24},{9,... | collective-permute-start | bytes 86024 | tf_op jit(solution)/shard_map/ppermute | solution.py:397
  46.0 8.9 %collective-permute-start.11 = (f32[56,128]{1,0:T(8,128)S(1)}, f32[56,128]{1,0:T(8,128)S(1)}, u32[]{:S(2)}, u32[]{:S(2)}) collective-permute-start(f32[56,128]{1,0:T(8,128)S(1)} %add.46), channel_id=1, source_target_pairs={{0,56},{1,57},{2,58},{3,59},{4,60},{5,61},{6,62},{7,63},{8,16},{9,... | collective-permute-start | bytes 86024 | tf_op jit(solution)/shard_map/ppermute | solution.py:397
  47.1 7.8 %collective-permute-start.12 = (f32[56,128]{1,0:T(8,128)S(1)}, f32[56,128]{1,0:T(8,128)S(1)}, u32[]{:S(2)}, u32[]{:S(2)}) collective-permute-start(f32[56,128]{1,0:T(8,128)S(1)} %add.46), channel_id=1, source_target_pairs={{0,40},{1,41},{2,42},{3,43},{4,44},{5,45},{6,46},{7,47},{8,32},{9,... | collective-permute-start | bytes 86024 | tf_op jit(solution)/shard_map/ppermute | solution.py:397
  49.3 15.6 %collective-permute-start.2 = (f32[512,128]{1,0:T(8,128)S(1)}, f32[512,128]{1,0:T(8,128)S(1)}, u32[]{:S(2)}, u32[]{:S(2)}) collective-permute-start(f32[512,128]{1,0:T(8,128)S(1)} %get-tuple-element.44), channel_id=1, source_target_pairs={{0,1},{1,0},{2,3},{3,2},{4,5},{5,4},{6,7},{7,6},{8,9},{9,8},{10,11... | collective-permute-start | bytes 786440 | tf_op jit(solution)/shard_map/ppermute | solution.py:397
  54.9 10.0 %collective-permute-start.3 = (f32[512,128]{1,0:T(8,128)S(1)}, f32[512,128]{1,0:T(8,128)S(1)}, u32[]{:S(2)}, u32[]{:S(2)}) collective-permute-start(f32[512,128]{1,0:T(8,128)S(1)} %get-tuple-element.45), channel_id=1, source_target_pairs={{0,255},{1,2},{2,1},{3,4},{4,3},{5,6},{6,5},{7,8},{8,7},{9,10},{10... | collective-permute-start | bytes 786440 | tf_op jit(solution)/shard_map/ppermute | solution.py:397
  54.9 8.6 %collective-permute-start.13 = (f32[56,128]{1,0:T(8,128)S(1)}, f32[56,128]{1,0:T(8,128)S(1)}, u32[]{:S(2)}, u32[]{:S(2)}) collective-permute-start(f32[56,128]{1,0:T(8,128)S(1)} %add_add_fusion.mine), channel_id=1, source_target_pairs={{0,1},{1,0},{2,3},{3,2},{4,5},{5,4},{6,7},{7,6},{8,9},{9,8},{10,11... | collective-permute-start | bytes 86024 | tf_op jit(solution)/shard_map/ppermute | solution.py:397
